TPU v7x, 32 devices: a whole 2x2x4 slice. The times are simulated.
32 devices in a mesh: qrow: 4 (over y, x), kcol: 8 (over z, core).
Axes of the slice: x: 2, y: 2, z: 4, core: 2. Of those that a mesh axis runs over, the one named last changes fastest.
Arguments:
- query: bfloat16 [4096, 1024], P('kcol', 'qrow'), may hold values from -6 to 6
- key: bfloat16 [4096, 256], P(('kcol', 'qrow')), may hold values from -6 to 6
- value: bfloat16 [4096, 256], P(('kcol', 'qrow')), may hold values from -6 to 6
- output: bfloat16 [4096, 1024], P('kcol', 'qrow'), may hold values from -6 to 6
- grad_out: bfloat16 [4096, 1024], P('kcol', 'qrow'), may hold values from -6 to 6
- lse: float32 [16, 4096], P('qrow', 'kcol'), may hold values from 2 to 5
- doc_ids: int32 [4096], replicated, may hold values from 0 to 7, never falling along the last dimension, each value on 1 to 3072 neighbouring positions
Outputs:
- grad_query: float32 [4096, 1024], P('kcol', 'qrow')
- grad_key: float32 [4096, 256], P(('kcol', 'qrow'))
- grad_value: float32 [4096, 256], P(('kcol', 'qrow'))
Inputs may be any that keep to these rules, and one draw needn't show every extreme that they name: `doc_ids`: document ids never fall along the sequence; no document is longer than 4096 // 2 + 2 * (512) tokens.
All inputs are finite; a program needn't handle non-finite values.
Results may differ from a plain program's by a relative error of at most 0.0058.
Values may be sent and summed in bfloat16 or wider, within the bound.
No kernel may reach another device: no remote copies, remote signals or barrier semaphores. Data moves between devices by JAX's collectives and lax.ppermute only.
A program may use at most 192 MiB of HBM per device.

v0:
```python
import functools
import jax
import jax.numpy as jnp
from jax import lax
from jax.experimental import pallas as pl
from jax.experimental.pallas import tpu as pltpu
from jax.sharding import PartitionSpec as P

HEAD_DIM = 64
GROUP = 4
DOCS = 16
FAR = 512.0
SUB = 256
EXTRA = 8
PACK = 56
LOG2E = 1.4426950408889634
SCORE_SCALE = 0.125

f32, bf16 = jnp.float32, jnp.bfloat16
VMEM_SPEC = pl.BlockSpec(memory_space=pltpu.VMEM)
SMEM_SPEC = pl.BlockSpec(memory_space=pltpu.SMEM)


def small(mib=4):
    return pltpu.CompilerParams(vmem_limit_bytes=mib << 20)


def nt(a, b):
    return lax.dot_general(a, b, (((1,), (1,)), ((), ())), preferred_element_type=f32)


def nn(a, b):
    return lax.dot_general(a, b, (((1,), (0,)), ((), ())), preferred_element_type=f32)


def halves_swapped(x):
    return jnp.concatenate([x[:, HEAD_DIM:], x[:, :HEAD_DIM]], axis=1)


def three(x):
    high = x.astype(bf16).astype(f32)
    rest = x - high
    middle = rest.astype(bf16).astype(f32)
    return high, middle, rest - middle


def one_hot_rows(doc_row, value):
    length = doc_row.shape[1]
    ids = lax.broadcasted_iota(jnp.int32, (DOCS, length), 0).astype(f32)
    return jnp.where(ids == doc_row, value, 0.0)


def pack_kernel(heads, place, key, value, *refs):
    pieces, stage = refs[:-1], refs[-1]
    for r in range(len(pieces)):
        g = r * heads // GROUP
        at = slice(g * HEAD_DIM, (g + 1) * HEAD_DIM)
        stage[r] = jnp.concatenate([key[:, at], value[:, at]], axis=1)
    for j, piece in enumerate(pieces):
        piece[...] = stage[place[0] ^ j]


def prep_kernel(query, grad_out, output, lse, packed):
    rows, feats = query.shape
    heads = feats // HEAD_DIM
    packed[:, :feats] = query[...]
    packed[:, feats : 2 * feats] = grad_out[...]
    product = grad_out[...].astype(f32) * output[...].astype(f32)
    high = product.astype(bf16)
    low = (product - high.astype(f32)).astype(bf16)
    head = lax.broadcasted_iota(jnp.int32, (feats, 128), 0) // HEAD_DIM
    spot = lax.broadcasted_iota(jnp.int32, (feats, 128), 1) - EXTRA * head
    pick = jnp.where((spot >= 3) & (spot < 6), -1.0, 0.0).astype(bf16)
    d0, d1, d2 = three(nn(high, pick) + nn(low, pick))
    table = []
    for h in range(heads):
        table += list(three(-FAR - lse[h : h + 1, :])) + [jnp.zeros((EXTRA - 3, rows), f32)]
    table.append(jnp.zeros((128 - EXTRA * heads, rows), f32))
    place = lax.broadcasted_iota(jnp.int32, (rows, 128), 1) % EXTRA
    delta = jnp.where(place == 3, d0, jnp.where(place == 4, d1, d2))
    packed[:, 2 * feats :] = (jnp.concatenate(table, axis=0).T + delta).astype(bf16)


def join_kernel(place, *refs):
    parts, out = refs[:-1], refs[-1]
    length = parts[0].shape[0]
    for j, part in enumerate(parts):
        out[pl.ds(pl.multiple_of((place[0] ^ j) * length, length), length), :] = part[...]


def expand_kernel(sides, panel, first, last, *refs):
    packs, docs = refs[:sides], refs[sides]
    q_ext, g_ext, q_t, g_t, docs_out = refs[sides + 1 :]
    docs_out[...] = docs[...]
    feats = q_t.shape[0]
    heads = feats // HEAD_DIM
    rows = docs.shape[1]
    lane = lax.broadcasted_iota(jnp.int32, (rows, 128), 1)
    low_half = lane < HEAD_DIM
    source = lax.broadcasted_iota(jnp.int32, (128, 128), 0)
    target = lax.broadcasted_iota(jnp.int32, (128, 128), 1)
    offset = target % HEAD_DIM
    for side, packed in enumerate(packs):
        dst = slice(side * rows, (side + 1) * rows)
        doc_row = docs[pl.ds(panel[side], 1), :].astype(f32)
        half = [jnp.zeros((3, rows), f32), one_hot_rows(doc_row, FAR), jnp.zeros((HEAD_DIM - 3 - DOCS, rows), f32)]
        spread = jnp.concatenate(half + half, axis=0).T
        extra = packed[:, 2 * feats :]
        for p in range(heads // 2):
            at = slice(p * 128, (p + 1) * 128)
            q_pair = packed[:, at].astype(f32) * SCORE_SCALE
            g_pair = packed[:, feats + p * 128 : feats + (p + 1) * 128].astype(f32)
            q_t[at, dst] = q_pair.T.astype(bf16)
            g_t[at, dst] = g_pair.T.astype(bf16)
            base = EXTRA * jnp.where(target < HEAD_DIM, 2 * p + 1, 2 * p)
            move_q = jnp.where((source == base + offset) & (offset < 3), 1.0, 0.0).astype(bf16)
            move_g = jnp.where((source == base + 3 + offset) & (offset < 3), 1.0, 0.0).astype(bf16)
            q_more = nn(extra, move_q) + spread
            g_more = nn(extra, move_g)
            q_ext[2 * p, dst, :] = jnp.where(low_half, q_pair, q_more).astype(bf16)
            q_ext[2 * p + 1, dst, :] = jnp.where(low_half, q_more, q_pair).astype(bf16)
            g_ext[2 * p, dst, :] = jnp.where(low_half, g_pair, g_more).astype(bf16)
            g_ext[2 * p + 1, dst, :] = jnp.where(low_half, g_more, g_pair).astype(bf16)


def band_kernel(shift, q_tile, chained, *refs):
    causal = shift == 0
    q_panel, first, last, q_ext, g_ext, q_t, g_t, docs, pair = refs[:9]
    refs = refs[9 + (1 if chained else 0) :]
    dq, out, *side, acc, k_ext, v_ext, k_lone = refs
    heads, q_rows, _ = q_ext.shape
    rows = pair.shape[0]
    subs = rows // SUB
    q_subs = q_tile // SUB
    per_panel = rows // q_tile
    q_tiles = q_panel.shape[0] * per_panel
    if not chained:
        dq[...] = jnp.zeros_like(dq)
    acc[...] = jnp.zeros_like(acc)

    def one(qt, kt, masked):
        at_q = pl.ds(pl.multiple_of(qt * q_tile, q_tile), q_tile)
        at_k = pl.ds(pl.multiple_of(kt * SUB, SUB), SUB)
        weights, score_grads = [], []
        if masked:
            ahead = (qt % per_panel) * q_tile - kt * SUB
            q_pos = lax.broadcasted_iota(jnp.int32, (q_tile, SUB), 0) + ahead
            live = lax.broadcasted_iota(jnp.int32, (q_tile, SUB), 1) <= q_pos
        for h in range(heads):
            weight = jnp.exp2(nt(q_ext[h, at_q, :], k_ext[h % 2, at_k, :]) * LOG2E)
            if masked:
                weight = jnp.where(live, weight, 0.0)
            grad = nt(g_ext[h, at_q, :], v_ext[h % 2, at_k, :])
            weights.append(weight.astype(bf16))
            score_grads.append((weight * grad).astype(bf16))
        key_sum = value_sum = 0.0
        for h in range(heads):
            at = slice(h * HEAD_DIM, (h + 1) * HEAD_DIM)
            key_sum += nn(q_t[at, at_q], score_grads[h])
            value_sum += nn(g_t[at, at_q], weights[h])
        for p in range(heads // 2):
            dq[at_q, p * 128 : (p + 1) * 128] += nn(score_grads[2 * p], k_lone[0, at_k, :]) + nn(
                score_grads[2 * p + 1], k_lone[1, at_k, :]
            )
        acc[:HEAD_DIM, at_k] += key_sum
        acc[HEAD_DIM:, at_k] += value_sum

    key_side = q_panel[0] - shift
    some = first[q_panel[0] * subs] <= last[jnp.maximum(key_side, 0) * subs + subs - 1]
    for j in range(1, q_panel.shape[0]):
        some = some | (first[q_panel[j] * subs] <= last[jnp.maximum(key_side, 0) * subs + subs - 1])
    some = some & (key_side >= 0)
    if causal:
        reach = key_side <= q_panel[0]
        for j in range(1, q_panel.shape[0]):
            reach = reach | (key_side <= q_panel[j])
        some = some & reach

    @pl.when(some)
    def _():
        lane = lax.broadcasted_iota(jnp.int32, (rows, 128), 1)
        low_half = lane < HEAD_DIM
        ones = jnp.where(lane % HEAD_DIM < 3, 1.0, 0.0)
        doc_row = docs[pl.ds(key_side, 1), :].astype(f32)
        half = [jnp.ones((3, rows), f32), one_hot_rows(doc_row, 1.0), jnp.zeros((HEAD_DIM - 3 - DOCS, rows), f32)]
        extra = jnp.concatenate(half + half, axis=0).T
        straight = pair[...].astype(f32)
        turned = halves_swapped(pair[...]).astype(f32)
        k_ext[0] = jnp.where(low_half, straight, extra).astype(bf16)
        k_ext[1] = jnp.where(low_half, extra, turned).astype(bf16)
        v_ext[0] = jnp.where(low_half, turned, ones).astype(bf16)
        v_ext[1] = jnp.where(low_half, ones, straight).astype(bf16)
        k_lone[0] = jnp.where(low_half, straight * SCORE_SCALE, 0.0).astype(bf16)
        k_lone[1] = jnp.where(low_half, 0.0, turned * SCORE_SCALE).astype(bf16)

        def step(index, carry):
            qt, kt = index // subs, index % subs
            q_at = q_panel[qt // per_panel] * subs + (qt % per_panel) * q_subs
            k_at = key_side * subs + kt
            live = first[q_at] <= last[k_at]
            if not causal:
                pl.when(live)(functools.partial(one, qt, kt, False))
            else:
                live = live & (k_at < q_at + q_subs)
                below = k_at < q_at
                pl.when(live & below)(functools.partial(one, qt, kt, False))
                pl.when(live & jnp.logical_not(below))(functools.partial(one, qt, kt, True))
            return carry

        lax.fori_loop(0, q_tiles * subs, step, 0)

    out[...] = acc[...].astype(out.dtype)
    if side:
        side[0][...] = dq[rows:, :].astype(bf16)


def collect_kernel(ways, place, *refs):
    parts, outs = refs[:-ways], refs[-ways:]
    chunk = outs[0].shape[1]
    for j, out in enumerate(outs):
        at = pl.ds(pl.multiple_of((place[0] ^ j) * chunk, chunk), chunk)
        total = parts[0][:, at]
        for part in parts[1:]:
            total = total + part[:, at].astype(f32)
        out[...] = total.astype(out.dtype)


def finish_kernel(ways, count, place, dq, *refs):
    chunks, (other,), (grad_query, grad_key, grad_value, got) = refs[:count], refs[count : count + 1], refs[count + 1 :]
    for j, chunk in enumerate(chunks):
        got[place[0] ^ j] = chunk[...].astype(f32)
    keys, values = [], []
    for g in range(count // ways):
        block = got[g * ways]
        for w in range(1, ways):
            block = block + got[g * ways + w]
        keys.append(block[:HEAD_DIM])
        values.append(block[HEAD_DIM:])
    grad_key[...] = jnp.concatenate(keys, axis=0).T
    grad_value[...] = jnp.concatenate(values, axis=0).T
    grad_query[...] = dq[: grad_query.shape[0], :] + other[...].astype(f32)


def per_device(query, key, value, output, grad_out, lse, doc_ids):
    row_count, col_count = lax.axis_size("qrow"), lax.axis_size("kcol")
    col = lax.axis_index("kcol")
    rows, feats = query.shape
    heads = feats // HEAD_DIM
    key_rows, key_feats = key.shape
    pair_feats = 2 * HEAD_DIM
    chips = col_count // 2

    def swap(x):
        return lax.ppermute(x, "kcol", [(i, i ^ 1) for i in range(col_count)])

    def up(x, d):
        return lax.ppermute(x, "kcol", [(i, i + 2 * d) for i in range(col_count - 2 * d)])

    def down(x, d):
        return lax.ppermute(x, "kcol", [(i + 2 * d, i) for i in range(col_count - 2 * d)])

    def across(x, j):
        return lax.ppermute(x, "qrow", [(i, i ^ j) for i in range(row_count)]) if j else x

    place = lax.axis_index("qrow").astype(jnp.int32)[None]
    pieces = pl.pallas_call(
        functools.partial(pack_kernel, heads),
        in_specs=[SMEM_SPEC] + [VMEM_SPEC] * 2,
        out_specs=[VMEM_SPEC] * row_count,
        out_shape=[jax.ShapeDtypeStruct((key_rows, pair_feats), bf16)] * row_count,
        scratch_shapes=[pltpu.VMEM((row_count, key_rows, pair_feats), bf16)],
        compiler_params=small(PACK),
        name="pack",
    )(place, key, value)
    packed = pl.pallas_call(
        prep_kernel,
        in_specs=[VMEM_SPEC] * 4,
        out_specs=VMEM_SPEC,
        out_shape=jax.ShapeDtypeStruct((rows, 2 * feats + 128), bf16),
        compiler_params=small(56),
        name="prep",
    )(query, grad_out, output, lse)
    pieces = [across(x, j) for j, x in enumerate(pieces)]
    source, *pieces = lax.optimization_barrier((packed, *pieces))
    packed_other = swap(source)

    docs = doc_ids.reshape(col_count, rows)
    first, last = docs[:, ::SUB].reshape(-1), docs[:, SUB - 1 :: SUB].reshape(-1)
    mine = jnp.stack([col, col ^ 1]).astype(jnp.int32)

    q_ext, g_ext, q_t, g_t, docs = pl.pallas_call(
        functools.partial(expand_kernel, 2),
        in_specs=[SMEM_SPEC] * 3 + [VMEM_SPEC] * 3,
        out_specs=[VMEM_SPEC] * 5,
        out_shape=[jax.ShapeDtypeStruct((heads, 2 * rows, 128), bf16)] * 2
        + [jax.ShapeDtypeStruct((feats, 2 * rows), bf16)] * 2
        + [jax.ShapeDtypeStruct(docs.shape, jnp.int32)],
        compiler_params=small(16),
        name="expand",
    )(mine, first, last, packed, packed_other, docs)
    pair = pl.pallas_call(
        join_kernel,
        in_specs=[SMEM_SPEC] + [VMEM_SPEC] * row_count,
        out_specs=VMEM_SPEC,
        out_shape=jax.ShapeDtypeStruct((rows, pair_feats), bf16),
        compiler_params=small(),
        name="join",
    )(place, *pieces)

    def band(name, shift, block, dq, q_tile, out_type):
        chained = dq is not None
        extra = [dq] if chained else []
        return pl.pallas_call(
            functools.partial(band_kernel, shift, q_tile, chained),
            in_specs=[SMEM_SPEC] * 3 + [VMEM_SPEC] * (6 + len(extra)),
            out_specs=[VMEM_SPEC] * (3 if shift == 2 else 2),
            out_shape=[
                jax.ShapeDtypeStruct((2 * rows, feats), f32),
                jax.ShapeDtypeStruct((pair_feats, rows), out_type),
            ]
            + ([jax.ShapeDtypeStruct((rows, feats), bf16)] if shift == 2 else []),
            scratch_shapes=[pltpu.VMEM((pair_feats, rows), f32)] + [pltpu.VMEM((2, rows, 128), bf16)] * 3,
            input_output_aliases={9: 0} if chained else {},
            compiler_params=small(24),
            cost_estimate=pl.CostEstimate(
                flops=20 * rows * rows * feats,
                bytes_accessed=6 << 20,
                transcendentals=2 * rows * rows * heads,
            ),
            name=name,
        )(mine, first, last, q_ext, g_ext, q_t, g_t, docs, block, *extra)

    reach = min(chips - 1, chips // 2 + 1)
    order = [*range(2, reach + 1), 1]
    blocks = {d: up(pair, d) for d in order[:-1]}
    dq, own = band("own", 0, pair, None, SUB, f32)
    late, own = lax.optimization_barrier((pair, own))
    blocks[1] = up(late, 1)
    back = []
    for d in order[:-1]:
        dq, grads = band(f"band{d}", 2 * d, blocks[d], dq, 2 * SUB if d < reach else SUB, bf16)
        back.append(down(grads, d))
    dq, grads, side = band("band1", 2, blocks[1], dq, 2 * SUB, bf16)
    back.append(down(grads, 1))
    side, *back = lax.optimization_barrier((side, *back))
    chunk = jax.ShapeDtypeStruct((pair_feats, key_rows), bf16)
    chunks = pl.pallas_call(
        functools.partial(collect_kernel, row_count),
        in_specs=[SMEM_SPEC] + [VMEM_SPEC] * (1 + len(back)),
        out_specs=[VMEM_SPEC] * row_count,
        out_shape=[chunk] * row_count,
        compiler_params=small(8),
        name="collect",
    )(place, own, *back)
    chunks = [across(x, j) for j, x in enumerate(chunks)]
    other = swap(side)
    return pl.pallas_call(
        functools.partial(finish_kernel, row_count * HEAD_DIM // key_feats, row_count),
        in_specs=[SMEM_SPEC] + [VMEM_SPEC] * (2 + row_count),
        out_specs=[VMEM_SPEC] * 3,
        out_shape=[jax.ShapeDtypeStruct((rows, feats), f32)]
        + [jax.ShapeDtypeStruct((key_rows, key_feats), f32)] * 2,
        scratch_shapes=[pltpu.VMEM((row_count, pair_feats, key_rows), f32)],
        compiler_params=small(8),
        name="finish",
    )(place, dq, *chunks, other)


def solution(mesh):
    return jax.shard_map(
        per_device,
        mesh=mesh,
        in_specs=(
            P("kcol", "qrow"),
            P(("kcol", "qrow"), None),
            P(("kcol", "qrow"), None),
            P("kcol", "qrow"),
            P("kcol", "qrow"),
            P("qrow", "kcol"),
            P(),
        ),
        out_specs=(P("kcol", "qrow"), P(("kcol", "qrow"), None), P(("kcol", "qrow"), None)),
        check_vma=False,
    )
```

profile of v0, /device:TPU:16, one launch (start us, length us, event | category | flops | bytes accessed | tf_op | source)
XLA Modules:
  0.0 54.0 jit_solution(16933483528439548820)
XLA Ops:
  0.6 1.6 %pack.1 = (bf16[128,128]{1,0:T(8,128)(2,1)}, bf16[128,128]{1,0:T(8,128)(2,1)}, bf16[128,128]{1,0:T(8,128)(2,1)}, bf16[128,128]{1,0:T(8,128)(2,1)}) custom-call(s32[1]{0:T(128)} %bitcast.place, bf16[128,256]{1,0:T(8,128)(2,1)} %key.1, bf16[128,256]{1,0:T(8,128)(2,1)} %value.1), custom_call_target="tpu_custom_call" | custom-call | tf_op jit(solution)/shard_map/pack/pallas_call | solution.py:266
  2.3 1.5 %collective-permute-start = (bf16[128,128]{1,0:T(8,128)(2,1)}, bf16[128,128]{1,0:T(8,128)(2,1)S(1)}, u32[]{:S(2)}, u32[]{:S(2)}) collective-permute-start(bf16[128,128]{1,0:T(8,128)(2,1)} %get-tuple-element.37), channel_id=1, source_target_pairs={{0,8},{8,0},{16,24},{24,16},{1,9},{9,1},{17,25},{25,17},{2,10},{10... | collective-permute-start | bytes 98312 | tf_op jit(solution)/shard_map/ppermute | solution.py:263
  3.7 1.5 %collective-permute-start.1 = (bf16[128,128]{1,0:T(8,128)(2,1)}, bf16[128,128]{1,0:T(8,128)(2,1)S(1)}, u32[]{:S(2)}, u32[]{:S(2)}) collective-permute-start(bf16[128,128]{1,0:T(8,128)(2,1)} %get-tuple-element.38), channel_id=1, source_target_pairs={{0,16},{8,24},{16,0},{24,8},{1,17},{9,25},{17,1},{25,9},{2,18},{10... | collective-permute-start | bytes 98312 | tf_op jit(solution)/shard_map/ppermute | solution.py:263
  5.3 0.0 copy-start.1
  5.3 0.5 collective-permute-start.2
  5.7 2.3 %prep.1.refs_0_ = bf16[512,640]{1,0:T(8,128)(2,1)} custom-call(bf16[512,256]{1,0:T(8,128)(2,1)} %query.1, bf16[512,256]{1,0:T(8,128)(2,1)} %grad_out.1, bf16[512,256]{1,0:T(8,128)(2,1)} %output.1, f32[4,512]{1,0:T(4,128)} %lse.1), custom_call_target="tpu_custom_call" | custom-call | tf_op jit(solution)/shard_map/prep/pallas_call | solution.py:275
  8.1 0.0 collective-permute-done.refs_1_
  8.1 0.0 collective-permute-done.1.refs_2_
  8.1 2.2 %collective-permute-done.2.refs_3_ = bf16[128,128]{1,0:T(8,128)(2,1)S(1)} collective-permute-done((bf16[128,128]{1,0:T(8,128)(2,1)}, bf16[128,128]{1,0:T(8,128)(2,1)S(1)}, u32[]{:S(2)}, u32[]{:S(2)}) %collective-permute-start.2) | collective-permute-done | bytes 32800 | tf_op jit(solution)/shard_map/ppermute | solution.py:263
  10.3 0.0 collective-permute-start.3
  10.3 0.0 copy-done.1
  10.3 0.0 copy-start.2
  10.3 1.3 %collective-permute-start.6 = (bf16[512,128]{1,0:T(8,128)(2,1)S(1)}, bf16[512,128]{1,0:T(8,128)(2,1)S(1)}, u32[]{:S(2)}, u32[]{:S(2)}) collective-permute-start(bf16[512,128]{1,0:T(8,128)(2,1)S(1)} %join.1.refs_8_), channel_id=1, source_target_pairs={{0,4},{1,5},{2,6},{3,7},{8,12},{9,13},{10,14},{11,15},{16,20},{17,... | collective-permute-start | bytes 393224 | tf_op jit(solution)/shard_map/ppermute | solution.py:257
  11.6 0.1 pad_add_fusion.panel.refs_0_
  11.7 0.0 copy-done.2
  11.7 0.1 slice.7
  11.8 0.1 slice.6
  11.9 0.1 reshape.17.last.refs_2_
  11.9 0.1 reshape.16.first.refs_1_
  12.0 0.7 %collective-permute-start.5 = (bf16[512,128]{1,0:T(8,128)(2,1)S(1)}, bf16[512,128]{1,0:T(8,128)(2,1)S(1)}, u32[]{:S(2)}, u32[]{:S(2)}) collective-permute-start(bf16[512,128]{1,0:T(8,128)(2,1)S(1)} %join.1.refs_8_), channel_id=1, source_target_pairs={{0,6},{1,7},{8,14},{9,15},{16,22},{17,23},{24,30},{25,31}} | collective-permute-start | bytes 393224 | tf_op jit(solution)/shard_map/ppermute | solution.py:257
  12.7 0.0 collective-permute-done.3.refs_1_
  12.7 0.0 copy-start
  12.7 1.1 %copy-done = bf16[512,640]{1,0:T(8,128)(2,1)S(1)} copy-done((bf16[512,640]{1,0:T(8,128)(2,1)S(1)}, bf16[512,640]{1,0:T(8,128)(2,1)}, u32[]{:S(2)}) %copy-start) | copy-done | bytes 655384
  13.8 1.4 %expand.1 = (bf16[4,1024,128]{2,1,0:T(8,128)(2,1)S(1)}, bf16[4,1024,128]{2,1,0:T(8,128)(2,1)S(1)}, bf16[256,1024]{1,0:T(8,128)(2,1)S(1)}, bf16[256,1024]{1,0:T(8,128)(2,1)S(1)}, s32[8,512]{1,0:T(8,128)S(1)}) custom-call(s32[2]{0:T(128)S(1)} %pad_add_fusion.panel.refs_0_, s32[16]{0:T(128)S(1)} %reshape.16.first.refs_1_, s32[16]{0:T(128)S(1)} %reshape.17.last.refs_2_, ...), custom_call_target="tpu_custom_call" | custom-call | tf_op jit(solution)/shard_map/expand/pallas_call | solution.py:291
  15.2 6.4 %own.1 = (f32[1024,256]{1,0:T(8,128)S(1)}, f32[128,512]{1,0:T(8,128)S(1)}) custom-call(s32[2]{0:T(128)S(1)} %pad_add_fusion.panel.refs_0_, s32[16]{0:T(128)S(1)} %reshape.16.first.refs_1_, s32[16]{0:T(128)S(1)} %reshape.17.last.refs_2_, bf16[4,1024,128]{2,1,0:T(8,128)(2,1)S(1)} %get-tuple-element.41.refs_3_, ...), custom_call_target="tpu_custom_call" | custom-call | flops 1342177280 | bytes 6291456 | tf_op jit(solution)/shard_map/own/pallas_call | solution.py:313
  21.6 4.1 %collective-permute-start.4 = (bf16[512,128]{1,0:T(8,128)(2,1)S(1)}, bf16[512,128]{1,0:T(8,128)(2,1)S(1)}, u32[]{:S(2)}, u32[]{:S(2)}) collective-permute-start(bf16[512,128]{1,0:T(8,128)(2,1)S(1)} %join.1.refs_8_), channel_id=1, source_target_pairs={{0,2},{1,3},{2,4},{3,5},{4,6},{5,7},{8,10},{9,11},{10,12},{11,13},... | collective-permute-start | bytes 393224 | tf_op jit(solution)/shard_map/ppermute | solution.py:257
  25.7 0.0 collective-permute-done.6.refs_8_
  25.8 0.6 %band2.1 = (f32[1024,256]{1,0:T(8,128)S(1)}, bf16[128,512]{1,0:T(8,128)(2,1)S(1)}) custom-call(s32[2]{0:T(128)S(1)} %pad_add_fusion.panel.refs_0_, s32[16]{0:T(128)S(1)} %reshape.16.first.refs_1_, s32[16]{0:T(128)S(1)} %reshape.17.last.refs_2_, bf16[4,1024,128]{2,1,0:T(8,128)(2,1)S(1)} %get-tuple-element.41.refs_3_, ...), custom_call_target="tpu_custom_call", output_to_operand_aliasing={{0}: (9, {})} | custom-call | flops 1342177280 | bytes 6291456 | tf_op jit(solution)/shard_map/band2/pallas_call | solution.py:313
  26.4 0.0 collective-permute-done.5.refs_8_
  26.4 0.6 %band3.1 = (f32[1024,256]{1,0:T(8,128)S(1)}, bf16[128,512]{1,0:T(8,128)(2,1)S(1)}) custom-call(s32[2]{0:T(128)S(1)} %pad_add_fusion.panel.refs_0_, s32[16]{0:T(128)S(1)} %reshape.16.first.refs_1_, s32[16]{0:T(128)S(1)} %reshape.17.last.refs_2_, bf16[4,1024,128]{2,1,0:T(8,128)(2,1)S(1)} %get-tuple-element.41.refs_3_, ...), custom_call_target="tpu_custom_call", output_to_operand_aliasing={{0}: (9, {})} | custom-call | flops 1342177280 | bytes 6291456 | tf_op jit(solution)/shard_map/band3/pallas_call | solution.py:313
  27.0 0.7 %collective-permute-start.8 = (bf16[128,512]{1,0:T(8,128)(2,1)S(1)}, bf16[128,512]{1,0:T(8,128)(2,1)S(1)}, u32[]{:S(2)}, u32[]{:S(2)}) collective-permute-start(bf16[128,512]{1,0:T(8,128)(2,1)S(1)} %get-tuple-element.59), channel_id=1, source_target_pairs={{6,0},{7,1},{14,8},{15,9},{22,16},{23,17},{30,24},{31,25}} | collective-permute-start | bytes 393224 | tf_op jit(solution)/shard_map/ppermute | solution.py:260
  27.6 5.4 %collective-permute-start.7 = (bf16[128,512]{1,0:T(8,128)(2,1)S(1)}, bf16[128,512]{1,0:T(8,128)(2,1)S(1)}, u32[]{:S(2)}, u32[]{:S(2)}) collective-permute-start(bf16[128,512]{1,0:T(8,128)(2,1)S(1)} %get-tuple-element.58), channel_id=1, source_target_pairs={{4,0},{5,1},{6,2},{7,3},{12,8},{13,9},{14,10},{15,11},{20,16},{21,... | collective-permute-start | bytes 393224 | tf_op jit(solution)/shard_map/ppermute | solution.py:260
  33.1 0.0 collective-permute-done.4.refs_8_
  33.1 6.3 %band1.1 = (f32[1024,256]{1,0:T(8,128)S(1)}, bf16[128,512]{1,0:T(8,128)(2,1)S(1)}, bf16[512,256]{1,0:T(8,128)(2,1)S(1)}) custom-call(s32[2]{0:T(128)S(1)} %pad_add_fusion.panel.refs_0_, s32[16]{0:T(128)S(1)} %reshape.16.first.refs_1_, s32[16]{0:T(128)S(1)} %reshape.17.last.refs_2_, ...), custom_call_target="tpu_custom_call", output_to_operand_aliasing={{0}: (9, {})} | custom-call | flops 1342177280 | bytes 6291456 | tf_op jit(solution)/shard_map/band1/pallas_call | solution.py:313
  39.4 1.9 %collective-permute-start.9 = (bf16[128,512]{1,0:T(8,128)(2,1)S(1)}, bf16[128,512]{1,0:T(8,128)(2,1)S(1)}, u32[]{:S(2)}, u32[]{:S(2)}) collective-permute-start(bf16[128,512]{1,0:T(8,128)(2,1)S(1)} %get-tuple-element.60), channel_id=1, source_target_pairs={{2,0},{3,1},{4,2},{5,3},{6,4},{7,5},{10,8},{11,9},{12,10},{13,11},... | collective-permute-start | bytes 393224 | tf_op jit(solution)/shard_map/ppermute | solution.py:260
  41.4 0.0 collective-permute-done.8.refs_2_
  41.4 1.0 %collective-permute-done.7.refs_1_ = bf16[128,512]{1,0:T(8,128)(2,1)S(1)} collective-permute-done((bf16[128,512]{1,0:T(8,128)(2,1)S(1)}, bf16[128,512]{1,0:T(8,128)(2,1)S(1)}, u32[]{:S(2)}, u32[]{:S(2)}) %collective-permute-start.7) | collective-permute-done | bytes 131104 | tf_op jit(solution)/shard_map/ppermute | solution.py:260
  42.4 4.6 %collective-permute-done.9.refs_3_ = bf16[128,512]{1,0:T(8,128)(2,1)S(1)} collective-permute-done((bf16[128,512]{1,0:T(8,128)(2,1)S(1)}, bf16[128,512]{1,0:T(8,128)(2,1)S(1)}, u32[]{:S(2)}, u32[]{:S(2)}) %collective-permute-start.9) | collective-permute-done | bytes 131104 | tf_op jit(solution)/shard_map/ppermute | solution.py:260
  47.0 0.0 collective-permute-start.13
  47.0 0.1 collect.1
  47.1 0.6 %collective-permute-start.10 = (bf16[128,128]{1,0:T(8,128)(2,1)S(1)}, bf16[128,128]{1,0:T(8,128)(2,1)S(1)}, u32[]{:S(2)}, u32[]{:S(2)}) collective-permute-start(bf16[128,128]{1,0:T(8,128)(2,1)S(1)} %get-tuple-element.65), channel_id=1, source_target_pairs={{0,8},{8,0},{16,24},{24,16},{1,9},{9,1},{17,25},{25,17},{2,10},{10... | collective-permute-start | bytes 98312 | tf_op jit(solution)/shard_map/ppermute | solution.py:263
  47.7 0.5 collective-permute-start.11
  48.2 2.5 %collective-permute-start.12 = (bf16[128,128]{1,0:T(8,128)(2,1)S(1)}, bf16[128,128]{1,0:T(8,128)(2,1)S(1)}, u32[]{:S(2)}, u32[]{:S(2)}) collective-permute-start(bf16[128,128]{1,0:T(8,128)(2,1)S(1)} %get-tuple-element.67), channel_id=1, source_target_pairs={{0,24},{8,16},{16,8},{24,0},{1,25},{9,17},{17,9},{25,1},{2,26},{10... | collective-permute-start | bytes 98312 | tf_op jit(solution)/shard_map/ppermute | solution.py:263
  50.6 0.4 collective-permute-done.10.refs_1_
  51.1 0.5 collective-permute-done.11.refs_2_
  51.6 1.4 %collective-permute-done.12.refs_3_ = bf16[128,128]{1,0:T(8,128)(2,1)S(1)} collective-permute-done((bf16[128,128]{1,0:T(8,128)(2,1)S(1)}, bf16[128,128]{1,0:T(8,128)(2,1)S(1)}, u32[]{:S(2)}, u32[]{:S(2)}) %collective-permute-start.12) | collective-permute-done | bytes 32800 | tf_op jit(solution)/shard_map/ppermute | solution.py:263
  53.0 0.0 collective-permute-done.13.refs_4_
  53.0 1.0 %finish.1 = (f32[512,256]{1,0:T(8,128)}, f32[128,256]{1,0:T(8,128)}, f32[128,256]{1,0:T(8,128)}) custom-call(s32[1]{0:T(128)} %bitcast.place, f32[1024,256]{1,0:T(8,128)S(1)} %get-tuple-element.55.dq, bf16[128,128]{1,0:T(8,128)(2,1)S(1)} %get-tuple-element.64.refs_0_, bf16[128,128]{1,0:T(8,128)(2,1)S(1)} %collective-permute-done.10.refs_1_, ...), custom_call_target="tpu_custom_call" | custom-call | tf_op jit(solution)/shard_map/finish/pallas_call | solution.py:357
  (2 shorter events, 0.0 us)
Async XLA Ops:
  2.3 5.8 %collective-permute-start = (bf16[128,128]{1,0:T(8,128)(2,1)}, bf16[128,128]{1,0:T(8,128)(2,1)S(1)}, u32[]{:S(2)}, u32[]{:S(2)}) collective-permute-start(bf16[128,128]{1,0:T(8,128)(2,1)} %get-tuple-element.37), channel_id=1, source_target_pairs={{0,8},{8,0},{16,24},{24,16},{1,9},{9,1},{17,25},{25,17},{2,10},{10... | collective-permute-start | bytes 98312 | tf_op jit(solution)/shard_map/ppermute | solution.py:263
  3.7 4.3 %collective-permute-start.1 = (bf16[128,128]{1,0:T(8,128)(2,1)}, bf16[128,128]{1,0:T(8,128)(2,1)S(1)}, u32[]{:S(2)}, u32[]{:S(2)}) collective-permute-start(bf16[128,128]{1,0:T(8,128)(2,1)} %get-tuple-element.38), channel_id=1, source_target_pairs={{0,16},{8,24},{16,0},{24,8},{1,17},{9,25},{17,1},{25,9},{2,18},{10... | collective-permute-start | bytes 98312 | tf_op jit(solution)/shard_map/ppermute | solution.py:263
  5.3 5.0 %copy-start.1 = (bf16[128,128]{1,0:T(8,128)(2,1)S(1)}, bf16[128,128]{1,0:T(8,128)(2,1)}, u32[]{:S(2)}) copy-start(bf16[128,128]{1,0:T(8,128)(2,1)} %get-tuple-element.46.refs_0_) | copy-start | bytes 98308
  5.3 5.0 %collective-permute-start.2 = (bf16[128,128]{1,0:T(8,128)(2,1)}, bf16[128,128]{1,0:T(8,128)(2,1)S(1)}, u32[]{:S(2)}, u32[]{:S(2)}) collective-permute-start(bf16[128,128]{1,0:T(8,128)(2,1)} %get-tuple-element.39), channel_id=1, source_target_pairs={{0,24},{8,16},{16,8},{24,0},{1,25},{9,17},{17,9},{25,1},{2,26},{10... | collective-permute-start | bytes 98312 | tf_op jit(solution)/shard_map/ppermute | solution.py:263
  10.3 2.4 %collective-permute-start.3 = (bf16[512,640]{1,0:T(8,128)(2,1)}, bf16[512,640]{1,0:T(8,128)(2,1)S(1)}, u32[]{:S(2)}, u32[]{:S(2)}) collective-permute-start(bf16[512,640]{1,0:T(8,128)(2,1)} %prep.1.refs_0_), channel_id=1, source_target_pairs={{0,1},{1,0},{2,3},{3,2},{4,5},{5,4},{6,7},{7,6},{8,9},{9,8},{10,11... | collective-permute-start | bytes 1966088 | tf_op jit(solution)/shard_map/ppermute | solution.py:254
  10.3 1.4 %copy-start.2 = (s32[4096]{0:T(1024)S(1)}, s32[4096]{0:T(1024)}, u32[]{:S(2)}) copy-start(s32[4096]{0:T(1024)} %param.13) | copy-start | bytes 49156
  10.3 15.4 %collective-permute-start.6 = (bf16[512,128]{1,0:T(8,128)(2,1)S(1)}, bf16[512,128]{1,0:T(8,128)(2,1)S(1)}, u32[]{:S(2)}, u32[]{:S(2)}) collective-permute-start(bf16[512,128]{1,0:T(8,128)(2,1)S(1)} %join.1.refs_8_), channel_id=1, source_target_pairs={{0,4},{1,5},{2,6},{3,7},{8,12},{9,13},{10,14},{11,15},{16,20},{17,... | collective-permute-start | bytes 393224 | tf_op jit(solution)/shard_map/ppermute | solution.py:257
  12.0 14.3 %collective-permute-start.5 = (bf16[512,128]{1,0:T(8,128)(2,1)S(1)}, bf16[512,128]{1,0:T(8,128)(2,1)S(1)}, u32[]{:S(2)}, u32[]{:S(2)}) collective-permute-start(bf16[512,128]{1,0:T(8,128)(2,1)S(1)} %join.1.refs_8_), channel_id=1, source_target_pairs={{0,6},{1,7},{8,14},{9,15},{16,22},{17,23},{24,30},{25,31}} | collective-permute-start | bytes 393224 | tf_op jit(solution)/shard_map/ppermute | solution.py:257
  12.7 1.1 %copy-start = (bf16[512,640]{1,0:T(8,128)(2,1)S(1)}, bf16[512,640]{1,0:T(8,128)(2,1)}, u32[]{:S(2)}) copy-start(bf16[512,640]{1,0:T(8,128)(2,1)} %prep.1.refs_0_) | copy-start | bytes 1966084
  21.6 11.5 %collective-permute-start.4 = (bf16[512,128]{1,0:T(8,128)(2,1)S(1)}, bf16[512,128]{1,0:T(8,128)(2,1)S(1)}, u32[]{:S(2)}, u32[]{:S(2)}) collective-permute-start(bf16[512,128]{1,0:T(8,128)(2,1)S(1)} %join.1.refs_8_), channel_id=1, source_target_pairs={{0,2},{1,3},{2,4},{3,5},{4,6},{5,7},{8,10},{9,11},{10,12},{11,13},... | collective-permute-start | bytes 393224 | tf_op jit(solution)/shard_map/ppermute | solution.py:257
  27.0 14.4 %collective-permute-start.8 = (bf16[128,512]{1,0:T(8,128)(2,1)S(1)}, bf16[128,512]{1,0:T(8,128)(2,1)S(1)}, u32[]{:S(2)}, u32[]{:S(2)}) collective-permute-start(bf16[128,512]{1,0:T(8,128)(2,1)S(1)} %get-tuple-element.59), channel_id=1, source_target_pairs={{6,0},{7,1},{14,8},{15,9},{22,16},{23,17},{30,24},{31,25}} | collective-permute-start | bytes 393224 | tf_op jit(solution)/shard_map/ppermute | solution.py:260
  27.6 14.8 %collective-permute-start.7 = (bf16[128,512]{1,0:T(8,128)(2,1)S(1)}, bf16[128,512]{1,0:T(8,128)(2,1)S(1)}, u32[]{:S(2)}, u32[]{:S(2)}) collective-permute-start(bf16[128,512]{1,0:T(8,128)(2,1)S(1)} %get-tuple-element.58), channel_id=1, source_target_pairs={{4,0},{5,1},{6,2},{7,3},{12,8},{13,9},{14,10},{15,11},{20,16},{21,... | collective-permute-start | bytes 393224 | tf_op jit(solution)/shard_map/ppermute | solution.py:260
  39.4 7.5 %collective-permute-start.9 = (bf16[128,512]{1,0:T(8,128)(2,1)S(1)}, bf16[128,512]{1,0:T(8,128)(2,1)S(1)}, u32[]{:S(2)}, u32[]{:S(2)}) collective-permute-start(bf16[128,512]{1,0:T(8,128)(2,1)S(1)} %get-tuple-element.60), channel_id=1, source_target_pairs={{2,0},{3,1},{4,2},{5,3},{6,4},{7,5},{10,8},{11,9},{12,10},{13,11},... | collective-permute-start | bytes 393224 | tf_op jit(solution)/shard_map/ppermute | solution.py:260
  47.0 6.0 %collective-permute-start.13 = (bf16[512,256]{1,0:T(8,128)(2,1)S(1)}, bf16[512,256]{1,0:T(8,128)(2,1)S(1)}, u32[]{:S(2)}, u32[]{:S(2)}) collective-permute-start(bf16[512,256]{1,0:T(8,128)(2,1)S(1)} %get-tuple-element.68), channel_id=1, source_target_pairs={{0,1},{1,0},{2,3},{3,2},{4,5},{5,4},{6,7},{7,6},{8,9},{9,8},{10,11... | collective-permute-start | bytes 786440 | tf_op jit(solution)/shard_map/ppermute | solution.py:254
  47.1 4.0 %collective-permute-start.10 = (bf16[128,128]{1,0:T(8,128)(2,1)S(1)}, bf16[128,128]{1,0:T(8,128)(2,1)S(1)}, u32[]{:S(2)}, u32[]{:S(2)}) collective-permute-start(bf16[128,128]{1,0:T(8,128)(2,1)S(1)} %get-tuple-element.65), channel_id=1, source_target_pairs={{0,8},{8,0},{16,24},{24,16},{1,9},{9,1},{17,25},{25,17},{2,10},{10... | collective-permute-start | bytes 98312 | tf_op jit(solution)/shard_map/ppermute | solution.py:263
  47.7 3.9 %collective-permute-start.11 = (bf16[128,128]{1,0:T(8,128)(2,1)S(1)}, bf16[128,128]{1,0:T(8,128)(2,1)S(1)}, u32[]{:S(2)}, u32[]{:S(2)}) collective-permute-start(bf16[128,128]{1,0:T(8,128)(2,1)S(1)} %get-tuple-element.66), channel_id=1, source_target_pairs={{0,16},{8,24},{16,0},{24,8},{1,17},{9,25},{17,1},{25,9},{2,18},{10... | collective-permute-start | bytes 98312 | tf_op jit(solution)/shard_map/ppermute | solution.py:263
  48.2 4.8 %collective-permute-start.12 = (bf16[128,128]{1,0:T(8,128)(2,1)S(1)}, bf16[128,128]{1,0:T(8,128)(2,1)S(1)}, u32[]{:S(2)}, u32[]{:S(2)}) collective-permute-start(bf16[128,128]{1,0:T(8,128)(2,1)S(1)} %get-tuple-element.67), channel_id=1, source_target_pairs={{0,24},{8,16},{16,8},{24,0},{1,25},{9,17},{17,9},{25,1},{2,26},{10... | collective-permute-start | bytes 98312 | tf_op jit(solution)/shard_map/ppermute | solution.py:263
where the time goes:
time: 54.4 us; the launch traced here: 54 us
  starting transfers between devices  21.2 us (39%)
  Pallas kernels  20.3 us (37%)
  waiting for transfers between devices  10.2 us (19%)
  local copies, waits for them, and re-layouts  1.4 us (3%)
  between operations  0.8 us (1%)
    pallas_call x4, Pallas kernels, band(): pl.pallas_call(functools.partial(band_kernel, shift, q_tile, chained), in...  13.9 us
    ppermute x3, starting transfers between devices, down(): lax.ppermute(x, 'kcol', [(i + 2 * d, i) for i in range(col_count - 2 * d)])  8.04 us
    ppermute x6, starting transfers between devices, across(): lax.ppermute(x, 'qrow', [(i, i ^ j) for i in range(row_count)])  7.04 us
    ppermute x3, starting transfers between devices, up(): lax.ppermute(x, 'kcol', [(i, i + 2 * d) for i in range(col_count - 2 * d)])  6.08 us
    ppermute x3, waiting for transfers between devices, down(): lax.ppermute(x, 'kcol', [(i + 2 * d, i) for i in range(col_count - 2 * d)])  5.61 us
    ppermute x6, waiting for transfers between devices, across(): lax.ppermute(x, 'qrow', [(i, i ^ j) for i in range(row_count)])  4.59 us
    pallas_call x1, Pallas kernels, per_device(): pl.pallas_call(prep_kernel, in_specs=[VMEM_SPEC] * 4, out_specs=VMEM_SPEC...  2.31 us
    pallas_call x1, Pallas kernels, per_device(): pl.pallas_call(functools.partial(pack_kernel, heads), in_specs=[SMEM_SPEC...  1.62 us
  transfers between devices with their start and end apart: 14, of which 6 were waited for; matrix products, arithmetic and copies ran while one was open for 1% of the time, Pallas kernels for 33%

commit v1 on v0

--- a/solution.py
+++ b/solution.py
@@ -123,7 +123,7 @@
             g_ext[2 * p + 1, dst, :] = jnp.where(low_half, g_more, g_pair).astype(bf16)
 
 
-def band_kernel(shift, q_tile, chained, *refs):
+def band_kernel(shift, q_tile, chained, only, *refs):
     causal = shift == 0
     q_panel, first, last, q_ext, g_ext, q_t, g_t, docs, pair = refs[:9]
     refs = refs[9 + (1 if chained else 0) :]
@@ -133,24 +133,26 @@
     subs = rows // SUB
     q_subs = q_tile // SUB
     per_panel = rows // q_tile
-    q_tiles = q_panel.shape[0] * per_panel
+    sides = range(2) if only is None else [only]
+    q_start, q_tiles = sides[0] * per_panel, len(sides) * per_panel
     if not chained:
         dq[...] = jnp.zeros_like(dq)
     acc[...] = jnp.zeros_like(acc)
 
-    def one(qt, kt, masked):
+    def one(qt, kt, masked, width=SUB):
         at_q = pl.ds(pl.multiple_of(qt * q_tile, q_tile), q_tile)
-        at_k = pl.ds(pl.multiple_of(kt * SUB, SUB), SUB)
+        at_k = pl.ds(pl.multiple_of(kt * SUB, SUB), width)
         weights, score_grads = [], []
         if masked:
             ahead = (qt % per_panel) * q_tile - kt * SUB
             q_pos = lax.broadcasted_iota(jnp.int32, (q_tile, SUB), 0) + ahead
             live = lax.broadcasted_iota(jnp.int32, (q_tile, SUB), 1) <= q_pos
-        for h in range(heads):
-            weight = jnp.exp2(nt(q_ext[h, at_q, :], k_ext[h % 2, at_k, :]) * LOG2E)
+        scores = [nt(q_ext[h, at_q, :], k_ext[h % 2, at_k, :]) for h in range(heads)]
+        grads = [nt(g_ext[h, at_q, :], v_ext[h % 2, at_k, :]) for h in range(heads)]
+        for score, grad in zip(scores, grads):
+            weight = jnp.exp2(score * LOG2E)
             if masked:
                 weight = jnp.where(live, weight, 0.0)
-            grad = nt(g_ext[h, at_q, :], v_ext[h % 2, at_k, :])
             weights.append(weight.astype(bf16))
             score_grads.append((weight * grad).astype(bf16))
         key_sum = value_sum = 0.0
@@ -166,15 +168,11 @@
         acc[HEAD_DIM:, at_k] += value_sum
 
     key_side = q_panel[0] - shift
-    some = first[q_panel[0] * subs] <= last[jnp.maximum(key_side, 0) * subs + subs - 1]
-    for j in range(1, q_panel.shape[0]):
-        some = some | (first[q_panel[j] * subs] <= last[jnp.maximum(key_side, 0) * subs + subs - 1])
+    key_end = last[jnp.maximum(key_side, 0) * subs + subs - 1]
+    some = False
+    for j in sides:
+        some = some | ((first[q_panel[j] * subs] <= key_end) & (key_side <= q_panel[j]))
     some = some & (key_side >= 0)
-    if causal:
-        reach = key_side <= q_panel[0]
-        for j in range(1, q_panel.shape[0]):
-            reach = reach | (key_side <= q_panel[j])
-        some = some & reach
 
     @pl.when(some)
     def _():
@@ -194,7 +192,7 @@
         k_lone[1] = jnp.where(low_half, 0.0, turned * SCORE_SCALE).astype(bf16)
 
         def step(index, carry):
-            qt, kt = index // subs, index % subs
+            qt, kt = q_start + index // subs, index % subs
             q_at = q_panel[qt // per_panel] * subs + (qt % per_panel) * q_subs
             k_at = key_side * subs + kt
             live = first[q_at] <= last[k_at]
@@ -207,7 +205,20 @@
                 pl.when(live & jnp.logical_not(below))(functools.partial(one, qt, kt, True))
             return carry
 
-        lax.fori_loop(0, q_tiles * subs, step, 0)
+        def wide(index, carry):
+            qt, kt = q_start + index // (subs // 2), 2 * (index % (subs // 2))
+            q_at = q_panel[qt // per_panel] * subs + (qt % per_panel) * q_subs
+            k_at = key_side * subs + kt
+            both = first[q_at] <= last[k_at]
+            after = jnp.logical_not(both) & (first[q_at] <= last[k_at + 1])
+            pl.when(both)(functools.partial(one, qt, kt, False, 2 * SUB))
+            pl.when(after)(functools.partial(one, qt, kt + 1, False))
+            return carry
+
+        if causal or q_subs == 1 or subs % 2:
+            lax.fori_loop(0, q_tiles * subs, step, 0)
+        else:
+            lax.fori_loop(0, q_tiles * subs // 2, wide, 0)
 
     out[...] = acc[...].astype(out.dtype)
     if side:
@@ -254,7 +265,7 @@
         return lax.ppermute(x, "kcol", [(i, i ^ 1) for i in range(col_count)])
 
     def up(x, d):
-        return lax.ppermute(x, "kcol", [(i, i + 2 * d) for i in range(col_count - 2 * d)])
+        return lax.ppermute(x, "kcol", [(i, (i + 2 * d) % col_count) for i in range(col_count)])
 
     def down(x, d):
         return lax.ppermute(x, "kcol", [(i + 2 * d, i) for i in range(col_count - 2 * d)])
@@ -307,18 +318,18 @@
         name="join",
     )(place, *pieces)
 
-    def band(name, shift, block, dq, q_tile, out_type):
+    def band(name, shift, block, dq, q_tile, side=None):
         chained = dq is not None
         extra = [dq] if chained else []
         return pl.pallas_call(
-            functools.partial(band_kernel, shift, q_tile, chained),
+            functools.partial(band_kernel, shift, q_tile, chained, side),
             in_specs=[SMEM_SPEC] * 3 + [VMEM_SPEC] * (6 + len(extra)),
-            out_specs=[VMEM_SPEC] * (3 if shift == 2 else 2),
+            out_specs=[VMEM_SPEC] * (3 if side == 1 else 2),
             out_shape=[
                 jax.ShapeDtypeStruct((2 * rows, feats), f32),
-                jax.ShapeDtypeStruct((pair_feats, rows), out_type),
+                jax.ShapeDtypeStruct((pair_feats, rows), f32 if shift == 0 else bf16),
             ]
-            + ([jax.ShapeDtypeStruct((rows, feats), bf16)] if shift == 2 else []),
+            + ([jax.ShapeDtypeStruct((rows, feats), bf16)] if side == 1 else []),
             scratch_shapes=[pltpu.VMEM((pair_feats, rows), f32)] + [pltpu.VMEM((2, rows, 128), bf16)] * 3,
             input_output_aliases={9: 0} if chained else {},
             compiler_params=small(24),
@@ -333,25 +344,26 @@
     reach = min(chips - 1, chips // 2 + 1)
     order = [*range(2, reach + 1), 1]
     blocks = {d: up(pair, d) for d in order[:-1]}
-    dq, own = band("own", 0, pair, None, SUB, f32)
+    dq, own = band("own", 0, pair, None, SUB, 0)
     late, own = lax.optimization_barrier((pair, own))
     blocks[1] = up(late, 1)
     back = []
-    for d in order[:-1]:
-        dq, grads = band(f"band{d}", 2 * d, blocks[d], dq, 2 * SUB if d < reach else SUB, bf16)
+    for d in order:
+        dq, grads = band(f"band{d}", 2 * d, blocks[d], dq, 2 * SUB if d < reach else SUB)
         back.append(down(grads, d))
-    dq, grads, side = band("band1", 2, blocks[1], dq, 2 * SUB, bf16)
-    back.append(down(grads, 1))
-    side, *back = lax.optimization_barrier((side, *back))
+    if reach > 1:
+        dq, back[-2] = lax.optimization_barrier((dq, back[-2]))
+    dq, more, side = band("rest", 0, pair, dq, 2 * SUB, 1)
+    side, more, *back = lax.optimization_barrier((side, more, *back))
     chunk = jax.ShapeDtypeStruct((pair_feats, key_rows), bf16)
     chunks = pl.pallas_call(
         functools.partial(collect_kernel, row_count),
-        in_specs=[SMEM_SPEC] + [VMEM_SPEC] * (1 + len(back)),
+        in_specs=[SMEM_SPEC] + [VMEM_SPEC] * (2 + len(back)),
         out_specs=[VMEM_SPEC] * row_count,
         out_shape=[chunk] * row_count,
         compiler_params=small(8),
         name="collect",
-    )(place, own, *back)
+    )(place, own, more, *back)
     chunks = [across(x, j) for j, x in enumerate(chunks)]
     other = swap(side)
     return pl.pallas_call(

time: 54.4 us -> 51.9 us (0.954)
  starting transfers between devices: 21.2 us -> 17 us
  waiting for transfers between devices: 10.2 us -> 11.4 us
    ppermute x3, starting transfers between devices: 6.08 us -> 3.29 us  [up(): lax.ppermute(x, 'kcol', [(i, (i + 2 * d) % col_count) for i in range(col_...]
    ppermute x3, starting transfers between devices: 8.04 us -> 6.7 us  [down(): lax.ppermute(x, 'kcol', [(i + 2 * d, i) for i in range(col_count - 2 * d)])]
    ppermute x3, waiting for transfers between devices: 5.61 us -> 6.81 us  [down(): lax.ppermute(x, 'kcol', [(i + 2 * d, i) for i in range(col_count - 2 * d)])]
    pallas_call x4 -> x5, Pallas kernels: 13.9 us -> 14.2 us  [band(): pl.pallas_call(functools.partial(band_kernel, shift, q_tile, chained, sid...]
  transfers between devices with their start and end apart: 14 -> 14, of which waited for: 6 -> 5; matrix products, arithmetic and copies ran while one was open for 1% -> 1% of each run, Pallas kernels for 33% -> 35%
where the time goes in v1:
time: 51.9 us; the launch traced here: 51.6 us
  Pallas kernels  20.7 us (40%)
  starting transfers between devices  17 us (33%)
  waiting for transfers between devices  11.4 us (22%)
  local copies, waits for them, and re-layouts  1.62 us (3%)
  between operations  0.77 us (1%)
    pallas_call x5, Pallas kernels, band(): pl.pallas_call(functools.partial(band_kernel, shift, q_tile, chained, sid...  14.2 us
    ppermute x6, starting transfers between devices, across(): lax.ppermute(x, 'qrow', [(i, i ^ j) for i in range(row_count)])  7.04 us
    ppermute x3, waiting for transfers between devices, down(): lax.ppermute(x, 'kcol', [(i + 2 * d, i) for i in range(col_count - 2 * d)])  6.81 us
    ppermute x3, starting transfers between devices, down(): lax.ppermute(x, 'kcol', [(i + 2 * d, i) for i in range(col_count - 2 * d)])  6.7 us
    ppermute x6, waiting for transfers between devices, across(): lax.ppermute(x, 'qrow', [(i, i ^ j) for i in range(row_count)])  4.6 us
    ppermute x3, starting transfers between devices, up(): lax.ppermute(x, 'kcol', [(i, (i + 2 * d) % col_count) for i in range(col_...  3.29 us
    pallas_call x1, Pallas kernels, per_device(): pl.pallas_call(prep_kernel, in_specs=[VMEM_SPEC] * 4, out_specs=VMEM_SPEC...  2.31 us
    pallas_call x1, Pallas kernels, per_device(): pl.pallas_call(functools.partial(pack_kernel, heads), in_specs=[SMEM_SPEC...  1.63 us
  transfers between devices with their start and end apart: 14, of which 5 were waited for; matrix products, arithmetic and copies ran while one was open for 1% of the time, Pallas kernels for 35%

profile of v1, /device:TPU:16, one launch (start us, length us, event | category | flops | bytes accessed | tf_op | source)
XLA Modules:
  0.0 51.6 jit_solution(1002092915816066812)
XLA Ops:
  0.6 1.6 %pack.1 = (bf16[128,128]{1,0:T(8,128)(2,1)}, bf16[128,128]{1,0:T(8,128)(2,1)}, bf16[128,128]{1,0:T(8,128)(2,1)}, bf16[128,128]{1,0:T(8,128)(2,1)}) custom-call(s32[1]{0:T(128)} %bitcast.place, bf16[128,256]{1,0:T(8,128)(2,1)} %key.1, bf16[128,256]{1,0:T(8,128)(2,1)} %value.1), custom_call_target="tpu_custom_call" | custom-call | tf_op jit(solution)/shard_map/pack/pallas_call | solution.py:277
  2.3 1.5 %collective-permute-start = (bf16[128,128]{1,0:T(8,128)(2,1)}, bf16[128,128]{1,0:T(8,128)(2,1)S(1)}, u32[]{:S(2)}, u32[]{:S(2)}) collective-permute-start(bf16[128,128]{1,0:T(8,128)(2,1)} %get-tuple-element.42), channel_id=1, source_target_pairs={{0,8},{8,0},{16,24},{24,16},{1,9},{9,1},{17,25},{25,17},{2,10},{10... | collective-permute-start | bytes 98312 | tf_op jit(solution)/shard_map/ppermute | solution.py:274
  3.8 1.5 %collective-permute-start.1 = (bf16[128,128]{1,0:T(8,128)(2,1)}, bf16[128,128]{1,0:T(8,128)(2,1)S(1)}, u32[]{:S(2)}, u32[]{:S(2)}) collective-permute-start(bf16[128,128]{1,0:T(8,128)(2,1)} %get-tuple-element.43), channel_id=1, source_target_pairs={{0,16},{8,24},{16,0},{24,8},{1,17},{9,25},{17,1},{25,9},{2,18},{10... | collective-permute-start | bytes 98312 | tf_op jit(solution)/shard_map/ppermute | solution.py:274
  5.3 0.0 copy-start.1
  5.3 0.5 collective-permute-start.2
  5.8 2.3 %prep.1.refs_0_ = bf16[512,640]{1,0:T(8,128)(2,1)} custom-call(bf16[512,256]{1,0:T(8,128)(2,1)} %query.1, bf16[512,256]{1,0:T(8,128)(2,1)} %grad_out.1, bf16[512,256]{1,0:T(8,128)(2,1)} %output.1, f32[4,512]{1,0:T(4,128)} %lse.1), custom_call_target="tpu_custom_call" | custom-call | tf_op jit(solution)/shard_map/prep/pallas_call | solution.py:286
  8.1 0.0 collective-permute-done.refs_1_
  8.1 0.0 collective-permute-done.1.refs_2_
  8.1 2.2 %collective-permute-done.2.refs_3_ = bf16[128,128]{1,0:T(8,128)(2,1)S(1)} collective-permute-done((bf16[128,128]{1,0:T(8,128)(2,1)}, bf16[128,128]{1,0:T(8,128)(2,1)S(1)}, u32[]{:S(2)}, u32[]{:S(2)}) %collective-permute-start.2) | collective-permute-done | bytes 32800 | tf_op jit(solution)/shard_map/ppermute | solution.py:274
  10.3 0.0 collective-permute-start.3
  10.3 0.0 copy-done.1
  10.3 0.4 collective-permute-start.6
  10.7 0.1 pad_add_fusion.panel.refs_0_
  10.8 0.2 copy-done.2
  11.0 0.1 slice.7
  11.1 0.1 slice.6
  11.2 0.1 reshape.17.last.refs_2_
  11.3 0.1 reshape.16.first.refs_1_
  11.3 2.5 %collective-permute-start.5 = (bf16[512,128]{1,0:T(8,128)(2,1)S(1)}, bf16[512,128]{1,0:T(8,128)(2,1)S(1)}, u32[]{:S(2)}, u32[]{:S(2)}) collective-permute-start(bf16[512,128]{1,0:T(8,128)(2,1)S(1)} %join.1.refs_8_), channel_id=1, source_target_pairs={{0,6},{1,7},{2,0},{3,1},{4,2},{5,3},{6,4},{7,5},{8,14},{9,15},{10,... | collective-permute-start | bytes 393224 | tf_op jit(solution)/shard_map/ppermute | solution.py:268
  13.8 0.0 collective-permute-done.3.refs_1_
  13.8 0.0 copy-start
  13.8 1.1 %copy-done = bf16[512,640]{1,0:T(8,128)(2,1)S(1)} copy-done((bf16[512,640]{1,0:T(8,128)(2,1)S(1)}, bf16[512,640]{1,0:T(8,128)(2,1)}, u32[]{:S(2)}) %copy-start) | copy-done | bytes 655384
  14.9 1.4 %expand.1 = (bf16[4,1024,128]{2,1,0:T(8,128)(2,1)S(1)}, bf16[4,1024,128]{2,1,0:T(8,128)(2,1)S(1)}, bf16[256,1024]{1,0:T(8,128)(2,1)S(1)}, bf16[256,1024]{1,0:T(8,128)(2,1)S(1)}, s32[8,512]{1,0:T(8,128)S(1)}) custom-call(s32[2]{0:T(128)S(1)} %pad_add_fusion.panel.refs_0_, s32[16]{0:T(128)S(1)} %reshape.16.first.refs_1_, s32[16]{0:T(128)S(1)} %reshape.17.last.refs_2_, ...), custom_call_target="tpu_custom_call" | custom-call | tf_op jit(solution)/shard_map/expand/pallas_call | solution.py:302
  16.3 3.3 %own.1 = (f32[1024,256]{1,0:T(8,128)S(1)}, f32[128,512]{1,0:T(8,128)S(1)}) custom-call(s32[2]{0:T(128)S(1)} %pad_add_fusion.panel.refs_0_, s32[16]{0:T(128)S(1)} %reshape.16.first.refs_1_, s32[16]{0:T(128)S(1)} %reshape.17.last.refs_2_, bf16[4,1024,128]{2,1,0:T(8,128)(2,1)S(1)} %get-tuple-element.46.refs_3_, ...), custom_call_target="tpu_custom_call" | custom-call | flops 1342177280 | bytes 6291456 | tf_op jit(solution)/shard_map/own/pallas_call | solution.py:324
  19.7 0.4 collective-permute-start.4
  20.1 0.0 collective-permute-done.6.refs_8_
  20.1 0.6 %band2.1 = (f32[1024,256]{1,0:T(8,128)S(1)}, bf16[128,512]{1,0:T(8,128)(2,1)S(1)}) custom-call(s32[2]{0:T(128)S(1)} %pad_add_fusion.panel.refs_0_, s32[16]{0:T(128)S(1)} %reshape.16.first.refs_1_, s32[16]{0:T(128)S(1)} %reshape.17.last.refs_2_, bf16[4,1024,128]{2,1,0:T(8,128)(2,1)S(1)} %get-tuple-element.46.refs_3_, ...), custom_call_target="tpu_custom_call", output_to_operand_aliasing={{0}: (9, {})} | custom-call | flops 1342177280 | bytes 6291456 | tf_op jit(solution)/shard_map/band2/pallas_call | solution.py:324
  20.7 0.0 collective-permute-done.5.refs_8_
  20.7 0.6 %band3.1 = (f32[1024,256]{1,0:T(8,128)S(1)}, bf16[128,512]{1,0:T(8,128)(2,1)S(1)}) custom-call(s32[2]{0:T(128)S(1)} %pad_add_fusion.panel.refs_0_, s32[16]{0:T(128)S(1)} %reshape.16.first.refs_1_, s32[16]{0:T(128)S(1)} %reshape.17.last.refs_2_, bf16[4,1024,128]{2,1,0:T(8,128)(2,1)S(1)} %get-tuple-element.46.refs_3_, ...), custom_call_target="tpu_custom_call", output_to_operand_aliasing={{0}: (9, {})} | custom-call | flops 1342177280 | bytes 6291456 | tf_op jit(solution)/shard_map/band3/pallas_call | solution.py:324
  21.3 0.7 %collective-permute-start.7 = (bf16[128,512]{1,0:T(8,128)(2,1)S(1)}, bf16[128,512]{1,0:T(8,128)(2,1)S(1)}, u32[]{:S(2)}, u32[]{:S(2)}) collective-permute-start(bf16[128,512]{1,0:T(8,128)(2,1)S(1)} %get-tuple-element.61), channel_id=1, source_target_pairs={{6,0},{7,1},{14,8},{15,9},{22,16},{23,17},{30,24},{31,25}} | collective-permute-start | bytes 393224 | tf_op jit(solution)/shard_map/ppermute | solution.py:271
  21.9 4.1 %collective-permute-start.8 = (bf16[128,512]{1,0:T(8,128)(2,1)S(1)}, bf16[128,512]{1,0:T(8,128)(2,1)S(1)}, u32[]{:S(2)}, u32[]{:S(2)}) collective-permute-start(bf16[128,512]{1,0:T(8,128)(2,1)S(1)} %get-tuple-element.67), channel_id=1, source_target_pairs={{4,0},{5,1},{6,2},{7,3},{12,8},{13,9},{14,10},{15,11},{20,16},{21,... | collective-permute-start | bytes 393224 | tf_op jit(solution)/shard_map/ppermute | solution.py:271
  26.0 0.0 collective-permute-done.4.refs_8_
  26.1 6.1 %band1.1 = (f32[1024,256]{1,0:T(8,128)S(1)}, bf16[128,512]{1,0:T(8,128)(2,1)S(1)}) custom-call(s32[2]{0:T(128)S(1)} %pad_add_fusion.panel.refs_0_, s32[16]{0:T(128)S(1)} %reshape.16.first.refs_1_, s32[16]{0:T(128)S(1)} %reshape.17.last.refs_2_, bf16[4,1024,128]{2,1,0:T(8,128)(2,1)S(1)} %get-tuple-element.46.refs_3_, ...), custom_call_target="tpu_custom_call", output_to_operand_aliasing={{0}: (9, {})} | custom-call | flops 1342177280 | bytes 6291456 | tf_op jit(solution)/shard_map/band1/pallas_call | solution.py:324
  32.2 1.9 %collective-permute-start.9 = (bf16[128,512]{1,0:T(8,128)(2,1)S(1)}, bf16[128,512]{1,0:T(8,128)(2,1)S(1)}, u32[]{:S(2)}, u32[]{:S(2)}) collective-permute-start(bf16[128,512]{1,0:T(8,128)(2,1)S(1)} %get-tuple-element.69), channel_id=1, source_target_pairs={{2,0},{3,1},{4,2},{5,3},{6,4},{7,5},{10,8},{11,9},{12,10},{13,11},... | collective-permute-start | bytes 393224 | tf_op jit(solution)/shard_map/ppermute | solution.py:271
  34.1 0.0 collective-permute-done.7.refs_3_
  34.1 3.6 %rest.1 = (f32[1024,256]{1,0:T(8,128)S(1)}, f32[128,512]{1,0:T(8,128)S(1)}, bf16[512,256]{1,0:T(8,128)(2,1)S(1)}) custom-call(s32[2]{0:T(128)S(1)} %pad_add_fusion.panel.refs_0_, s32[16]{0:T(128)S(1)} %reshape.16.first.refs_1_, s32[16]{0:T(128)S(1)} %reshape.17.last.refs_2_, ...), custom_call_target="tpu_custom_call", output_to_operand_aliasing={{0}: (9, {})} | custom-call | flops 1342177280 | bytes 6291456 | tf_op jit(solution)/shard_map/rest/pallas_call | solution.py:324
  37.7 0.0 collective-permute-done.8.refs_2_
  37.7 6.8 %collective-permute-done.9.refs_4_ = bf16[128,512]{1,0:T(8,128)(2,1)S(1)} collective-permute-done((bf16[128,512]{1,0:T(8,128)(2,1)S(1)}, bf16[128,512]{1,0:T(8,128)(2,1)S(1)}, u32[]{:S(2)}, u32[]{:S(2)}) %collective-permute-start.9) | collective-permute-done | bytes 131104 | tf_op jit(solution)/shard_map/ppermute | solution.py:271
  44.5 0.0 collective-permute-start.13
  44.5 0.1 collect.1
  44.7 0.6 %collective-permute-start.10 = (bf16[128,128]{1,0:T(8,128)(2,1)S(1)}, bf16[128,128]{1,0:T(8,128)(2,1)S(1)}, u32[]{:S(2)}, u32[]{:S(2)}) collective-permute-start(bf16[128,128]{1,0:T(8,128)(2,1)S(1)} %get-tuple-element.75), channel_id=1, source_target_pairs={{0,8},{8,0},{16,24},{24,16},{1,9},{9,1},{17,25},{25,17},{2,10},{10... | collective-permute-start | bytes 98312 | tf_op jit(solution)/shard_map/ppermute | solution.py:274
  45.3 0.5 collective-permute-start.11
  45.8 2.4 %collective-permute-start.12 = (bf16[128,128]{1,0:T(8,128)(2,1)S(1)}, bf16[128,128]{1,0:T(8,128)(2,1)S(1)}, u32[]{:S(2)}, u32[]{:S(2)}) collective-permute-start(bf16[128,128]{1,0:T(8,128)(2,1)S(1)} %get-tuple-element.77), channel_id=1, source_target_pairs={{0,24},{8,16},{16,8},{24,0},{1,25},{9,17},{17,9},{25,1},{2,26},{10... | collective-permute-start | bytes 98312 | tf_op jit(solution)/shard_map/ppermute | solution.py:274
  48.2 0.4 collective-permute-done.10.refs_1_
  48.6 0.5 %collective-permute-done.11.refs_2_ = bf16[128,128]{1,0:T(8,128)(2,1)S(1)} collective-permute-done((bf16[128,128]{1,0:T(8,128)(2,1)S(1)}, bf16[128,128]{1,0:T(8,128)(2,1)S(1)}, u32[]{:S(2)}, u32[]{:S(2)}) %collective-permute-start.11) | collective-permute-done | bytes 32800 | tf_op jit(solution)/shard_map/ppermute | solution.py:274
  49.2 1.4 %collective-permute-done.12.refs_3_ = bf16[128,128]{1,0:T(8,128)(2,1)S(1)} collective-permute-done((bf16[128,128]{1,0:T(8,128)(2,1)S(1)}, bf16[128,128]{1,0:T(8,128)(2,1)S(1)}, u32[]{:S(2)}, u32[]{:S(2)}) %collective-permute-start.12) | collective-permute-done | bytes 32800 | tf_op jit(solution)/shard_map/ppermute | solution.py:274
  50.6 0.0 collective-permute-done.13.refs_4_
  50.6 1.0 %finish.1 = (f32[512,256]{1,0:T(8,128)}, f32[128,256]{1,0:T(8,128)}, f32[128,256]{1,0:T(8,128)}) custom-call(s32[1]{0:T(128)} %bitcast.place, f32[1024,256]{1,0:T(8,128)S(1)} %get-tuple-element.63.dq, bf16[128,128]{1,0:T(8,128)(2,1)S(1)} %get-tuple-element.74.refs_0_, bf16[128,128]{1,0:T(8,128)(2,1)S(1)} %collective-permute-done.10.refs_1_, ...), custom_call_target="tpu_custom_call" | custom-call | tf_op jit(solution)/shard_map/finish/pallas_call | solution.py:369
  (3 shorter events, 0.0 us)
Async XLA Ops:
  2.3 5.8 %collective-permute-start = (bf16[128,128]{1,0:T(8,128)(2,1)}, bf16[128,128]{1,0:T(8,128)(2,1)S(1)}, u32[]{:S(2)}, u32[]{:S(2)}) collective-permute-start(bf16[128,128]{1,0:T(8,128)(2,1)} %get-tuple-element.42), channel_id=1, source_target_pairs={{0,8},{8,0},{16,24},{24,16},{1,9},{9,1},{17,25},{25,17},{2,10},{10... | collective-permute-start | bytes 98312 | tf_op jit(solution)/shard_map/ppermute | solution.py:274
  3.8 4.3 %collective-permute-start.1 = (bf16[128,128]{1,0:T(8,128)(2,1)}, bf16[128,128]{1,0:T(8,128)(2,1)S(1)}, u32[]{:S(2)}, u32[]{:S(2)}) collective-permute-start(bf16[128,128]{1,0:T(8,128)(2,1)} %get-tuple-element.43), channel_id=1, source_target_pairs={{0,16},{8,24},{16,0},{24,8},{1,17},{9,25},{17,1},{25,9},{2,18},{10... | collective-permute-start | bytes 98312 | tf_op jit(solution)/shard_map/ppermute | solution.py:274
  5.3 5.0 %copy-start.1 = (bf16[128,128]{1,0:T(8,128)(2,1)S(1)}, bf16[128,128]{1,0:T(8,128)(2,1)}, u32[]{:S(2)}) copy-start(bf16[128,128]{1,0:T(8,128)(2,1)} %get-tuple-element.51.refs_0_) | copy-start | bytes 98308
  5.3 5.0 %collective-permute-start.2 = (bf16[128,128]{1,0:T(8,128)(2,1)}, bf16[128,128]{1,0:T(8,128)(2,1)S(1)}, u32[]{:S(2)}, u32[]{:S(2)}) collective-permute-start(bf16[128,128]{1,0:T(8,128)(2,1)} %get-tuple-element.44), channel_id=1, source_target_pairs={{0,24},{8,16},{16,8},{24,0},{1,25},{9,17},{17,9},{25,1},{2,26},{10... | collective-permute-start | bytes 98312 | tf_op jit(solution)/shard_map/ppermute | solution.py:274
  10.3 3.5 %collective-permute-start.3 = (bf16[512,640]{1,0:T(8,128)(2,1)}, bf16[512,640]{1,0:T(8,128)(2,1)S(1)}, u32[]{:S(2)}, u32[]{:S(2)}) collective-permute-start(bf16[512,640]{1,0:T(8,128)(2,1)} %prep.1.refs_0_), channel_id=1, source_target_pairs={{0,1},{1,0},{2,3},{3,2},{4,5},{5,4},{6,7},{7,6},{8,9},{9,8},{10,11... | collective-permute-start | bytes 1966088 | tf_op jit(solution)/shard_map/ppermute | solution.py:265
  10.3 0.7 %copy-start.2 = (s32[4096]{0:T(1024)S(1)}, s32[4096]{0:T(1024)}, u32[]{:S(2)}) copy-start(s32[4096]{0:T(1024)} %param.13) | copy-start | bytes 49156
  10.3 9.7 %collective-permute-start.6 = (bf16[512,128]{1,0:T(8,128)(2,1)S(1)}, bf16[512,128]{1,0:T(8,128)(2,1)S(1)}, u32[]{:S(2)}, u32[]{:S(2)}) collective-permute-start(bf16[512,128]{1,0:T(8,128)(2,1)S(1)} %join.1.refs_8_), channel_id=1, source_target_pairs={{0,4},{1,5},{2,6},{3,7},{4,0},{5,1},{6,2},{7,3},{8,12},{9,13},{10,... | collective-permute-start | bytes 393224 | tf_op jit(solution)/shard_map/ppermute | solution.py:268
  11.3 9.3 %collective-permute-start.5 = (bf16[512,128]{1,0:T(8,128)(2,1)S(1)}, bf16[512,128]{1,0:T(8,128)(2,1)S(1)}, u32[]{:S(2)}, u32[]{:S(2)}) collective-permute-start(bf16[512,128]{1,0:T(8,128)(2,1)S(1)} %join.1.refs_8_), channel_id=1, source_target_pairs={{0,6},{1,7},{2,0},{3,1},{4,2},{5,3},{6,4},{7,5},{8,14},{9,15},{10,... | collective-permute-start | bytes 393224 | tf_op jit(solution)/shard_map/ppermute | solution.py:268
  13.8 1.1 %copy-start = (bf16[512,640]{1,0:T(8,128)(2,1)S(1)}, bf16[512,640]{1,0:T(8,128)(2,1)}, u32[]{:S(2)}) copy-start(bf16[512,640]{1,0:T(8,128)(2,1)} %prep.1.refs_0_) | copy-start | bytes 1966084
  19.7 6.4 %collective-permute-start.4 = (bf16[512,128]{1,0:T(8,128)(2,1)S(1)}, bf16[512,128]{1,0:T(8,128)(2,1)S(1)}, u32[]{:S(2)}, u32[]{:S(2)}) collective-permute-start(bf16[512,128]{1,0:T(8,128)(2,1)S(1)} %join.1.refs_8_), channel_id=1, source_target_pairs={{0,2},{1,3},{2,4},{3,5},{4,6},{5,7},{6,0},{7,1},{8,10},{9,11},{10,... | collective-permute-start | bytes 393224 | tf_op jit(solution)/shard_map/ppermute | solution.py:268
  21.3 12.8 %collective-permute-start.7 = (bf16[128,512]{1,0:T(8,128)(2,1)S(1)}, bf16[128,512]{1,0:T(8,128)(2,1)S(1)}, u32[]{:S(2)}, u32[]{:S(2)}) collective-permute-start(bf16[128,512]{1,0:T(8,128)(2,1)S(1)} %get-tuple-element.61), channel_id=1, source_target_pairs={{6,0},{7,1},{14,8},{15,9},{22,16},{23,17},{30,24},{31,25}} | collective-permute-start | bytes 393224 | tf_op jit(solution)/shard_map/ppermute | solution.py:271
  21.9 15.8 %collective-permute-start.8 = (bf16[128,512]{1,0:T(8,128)(2,1)S(1)}, bf16[128,512]{1,0:T(8,128)(2,1)S(1)}, u32[]{:S(2)}, u32[]{:S(2)}) collective-permute-start(bf16[128,512]{1,0:T(8,128)(2,1)S(1)} %get-tuple-element.67), channel_id=1, source_target_pairs={{4,0},{5,1},{6,2},{7,3},{12,8},{13,9},{14,10},{15,11},{20,16},{21,... | collective-permute-start | bytes 393224 | tf_op jit(solution)/shard_map/ppermute | solution.py:271
  32.2 12.4 %collective-permute-start.9 = (bf16[128,512]{1,0:T(8,128)(2,1)S(1)}, bf16[128,512]{1,0:T(8,128)(2,1)S(1)}, u32[]{:S(2)}, u32[]{:S(2)}) collective-permute-start(bf16[128,512]{1,0:T(8,128)(2,1)S(1)} %get-tuple-element.69), channel_id=1, source_target_pairs={{2,0},{3,1},{4,2},{5,3},{6,4},{7,5},{10,8},{11,9},{12,10},{13,11},... | collective-permute-start | bytes 393224 | tf_op jit(solution)/shard_map/ppermute | solution.py:271
  44.5 6.1 %collective-permute-start.13 = (bf16[512,256]{1,0:T(8,128)(2,1)S(1)}, bf16[512,256]{1,0:T(8,128)(2,1)S(1)}, u32[]{:S(2)}, u32[]{:S(2)}) collective-permute-start(bf16[512,256]{1,0:T(8,128)(2,1)S(1)} %get-tuple-element.78), channel_id=1, source_target_pairs={{0,1},{1,0},{2,3},{3,2},{4,5},{5,4},{6,7},{7,6},{8,9},{9,8},{10,11... | collective-permute-start | bytes 786440 | tf_op jit(solution)/shard_map/ppermute | solution.py:265
  44.7 4.0 %collective-permute-start.10 = (bf16[128,128]{1,0:T(8,128)(2,1)S(1)}, bf16[128,128]{1,0:T(8,128)(2,1)S(1)}, u32[]{:S(2)}, u32[]{:S(2)}) collective-permute-start(bf16[128,128]{1,0:T(8,128)(2,1)S(1)} %get-tuple-element.75), channel_id=1, source_target_pairs={{0,8},{8,0},{16,24},{24,16},{1,9},{9,1},{17,25},{25,17},{2,10},{10... | collective-permute-start | bytes 98312 | tf_op jit(solution)/shard_map/ppermute | solution.py:274
  45.3 3.9 %collective-permute-start.11 = (bf16[128,128]{1,0:T(8,128)(2,1)S(1)}, bf16[128,128]{1,0:T(8,128)(2,1)S(1)}, u32[]{:S(2)}, u32[]{:S(2)}) collective-permute-start(bf16[128,128]{1,0:T(8,128)(2,1)S(1)} %get-tuple-element.76), channel_id=1, source_target_pairs={{0,16},{8,24},{16,0},{24,8},{1,17},{9,25},{17,1},{25,9},{2,18},{10... | collective-permute-start | bytes 98312 | tf_op jit(solution)/shard_map/ppermute | solution.py:274
  45.8 4.8 %collective-permute-start.12 = (bf16[128,128]{1,0:T(8,128)(2,1)S(1)}, bf16[128,128]{1,0:T(8,128)(2,1)S(1)}, u32[]{:S(2)}, u32[]{:S(2)}) collective-permute-start(bf16[128,128]{1,0:T(8,128)(2,1)S(1)} %get-tuple-element.77), channel_id=1, source_target_pairs={{0,24},{8,16},{16,8},{24,0},{1,25},{9,17},{17,9},{25,1},{2,26},{10... | collective-permute-start | bytes 98312 | tf_op jit(solution)/shard_map/ppermute | solution.py:274

commit v2 on v1

--- a/solution.py
+++ b/solution.py
@@ -123,11 +123,25 @@
             g_ext[2 * p + 1, dst, :] = jnp.where(low_half, g_more, g_pair).astype(bf16)
 
 
-def band_kernel(shift, q_tile, chained, only, *refs):
+def band_kernel(shifts, q_tiles_by, chained, only, *refs):
+    count = len(shifts)
+    q_panel, first, last, q_ext, g_ext, q_t, g_t, docs = refs[:8]
+    pairs = refs[8 : 8 + count]
+    refs = refs[8 + count + (1 if chained else 0) :]
+    dq, outs, refs = refs[0], refs[1 : 1 + count], refs[1 + count :]
+    *side, acc, k_ext, v_ext, k_lone = refs
+    if not chained:
+        dq[...] = jnp.zeros_like(dq)
+    operands = (q_panel, first, last, q_ext, g_ext, q_t, g_t, docs)
+    for shift, q_tile, pair, out in zip(shifts, q_tiles_by, pairs, outs):
+        one_band(shift, q_tile, only, operands, pair, dq, out, acc, k_ext, v_ext, k_lone)
+    if side:
+        side[0][...] = dq[pairs[0].shape[0] :, :].astype(bf16)
+
+
+def one_band(shift, q_tile, only, operands, pair, dq, out, acc, k_ext, v_ext, k_lone):
     causal = shift == 0
-    q_panel, first, last, q_ext, g_ext, q_t, g_t, docs, pair = refs[:9]
-    refs = refs[9 + (1 if chained else 0) :]
-    dq, out, *side, acc, k_ext, v_ext, k_lone = refs
+    q_panel, first, last, q_ext, g_ext, q_t, g_t, docs = operands
     heads, q_rows, _ = q_ext.shape
     rows = pair.shape[0]
     subs = rows // SUB
@@ -135,8 +149,6 @@
     per_panel = rows // q_tile
     sides = range(2) if only is None else [only]
     q_start, q_tiles = sides[0] * per_panel, len(sides) * per_panel
-    if not chained:
-        dq[...] = jnp.zeros_like(dq)
     acc[...] = jnp.zeros_like(acc)
 
     def one(qt, kt, masked, width=SUB):
@@ -221,8 +233,6 @@
             lax.fori_loop(0, q_tiles * subs // 2, wide, 0)
 
     out[...] = acc[...].astype(out.dtype)
-    if side:
-        side[0][...] = dq[rows:, :].astype(bf16)
 
 
 def collect_kernel(ways, place, *refs):
@@ -318,42 +328,47 @@
         name="join",
     )(place, *pieces)
 
-    def band(name, shift, block, dq, q_tile, side=None):
+    def band(name, shifts, held, dq, q_sizes, side=None):
         chained = dq is not None
         extra = [dq] if chained else []
+        count = len(shifts)
         return pl.pallas_call(
-            functools.partial(band_kernel, shift, q_tile, chained, side),
-            in_specs=[SMEM_SPEC] * 3 + [VMEM_SPEC] * (6 + len(extra)),
-            out_specs=[VMEM_SPEC] * (3 if side == 1 else 2),
-            out_shape=[
-                jax.ShapeDtypeStruct((2 * rows, feats), f32),
-                jax.ShapeDtypeStruct((pair_feats, rows), f32 if shift == 0 else bf16),
-            ]
+            functools.partial(band_kernel, shifts, q_sizes, chained, side),
+            in_specs=[SMEM_SPEC] * 3 + [VMEM_SPEC] * (5 + count + len(extra)),
+            out_specs=[VMEM_SPEC] * (1 + count + (1 if side == 1 else 0)),
+            out_shape=[jax.ShapeDtypeStruct((2 * rows, feats), f32)]
+            + [jax.ShapeDtypeStruct((pair_feats, rows), bf16 if x else f32) for x in shifts]
             + ([jax.ShapeDtypeStruct((rows, feats), bf16)] if side == 1 else []),
             scratch_shapes=[pltpu.VMEM((pair_feats, rows), f32)] + [pltpu.VMEM((2, rows, 128), bf16)] * 3,
-            input_output_aliases={9: 0} if chained else {},
+            input_output_aliases={8 + count: 0} if chained else {},
             compiler_params=small(24),
             cost_estimate=pl.CostEstimate(
-                flops=20 * rows * rows * feats,
+                flops=20 * rows * rows * feats * count,
                 bytes_accessed=6 << 20,
-                transcendentals=2 * rows * rows * heads,
+                transcendentals=2 * rows * rows * heads * count,
             ),
             name=name,
-        )(mine, first, last, q_ext, g_ext, q_t, g_t, docs, block, *extra)
+        )(mine, first, last, q_ext, g_ext, q_t, g_t, docs, *held, *extra)
 
     reach = min(chips - 1, chips // 2 + 1)
     order = [*range(2, reach + 1), 1]
     blocks = {d: up(pair, d) for d in order[:-1]}
-    dq, own = band("own", 0, pair, None, SUB, 0)
+    dq, own = band("own", [0], [pair], None, [SUB], 0)
     late, own = lax.optimization_barrier((pair, own))
     blocks[1] = up(late, 1)
     back = []
-    for d in order:
-        dq, grads = band(f"band{d}", 2 * d, blocks[d], dq, 2 * SUB if d < reach else SUB)
-        back.append(down(grads, d))
+    sizes = {d: 2 * SUB if d < reach else SUB for d in order}
+    if reach > 1:
+        far = order[:-1]
+        dq, *grads = band(
+            "far", [2 * d for d in far], [blocks[d] for d in far], dq, [sizes[d] for d in far]
+        )
+        back += [down(x, d) for x, d in zip(grads, far)]
+    dq, grads = band("near", [2], [blocks[1]], dq, [sizes[1]])
+    back.append(down(grads, 1))
     if reach > 1:
         dq, back[-2] = lax.optimization_barrier((dq, back[-2]))
-    dq, more, side = band("rest", 0, pair, dq, 2 * SUB, 1)
+    dq, more, side = band("rest", [0], [pair], dq, [2 * SUB], 1)
     side, more, *back = lax.optimization_barrier((side, more, *back))
     chunk = jax.ShapeDtypeStruct((pair_feats, key_rows), bf16)
     chunks = pl.pallas_call(

time: 51.9 us -> 53.5 us (1.031); the launches traced: 51.6 us -> 52.5 us
  starting transfers between devices: 17 us -> 20.7 us
  waiting for transfers between devices: 11.4 us -> 9.47 us
  Pallas kernels: 20.7 us -> 20.1 us
    ppermute x3, waiting for transfers between devices: 6.81 us -> 4.39 us  [down(): lax.ppermute(x, 'kcol', [(i + 2 * d, i) for i in range(col_count - 2 * d)])]
    ppermute x2, starting transfers between devices: 0.01 us -> 1.92 us  [swap(): return lax.ppermute(x, 'kcol', [(i, i ^ 1) for i in range(col_count)])]
    ppermute x3, starting transfers between devices: 6.7 us -> 7.67 us  [down(): lax.ppermute(x, 'kcol', [(i + 2 * d, i) for i in range(col_count - 2 * d)])]
    ppermute x3, starting transfers between devices: 3.29 us -> 4.05 us  [up(): lax.ppermute(x, 'kcol', [(i, (i + 2 * d) % col_count) for i in range(col_...]
    pallas_call x5 -> x4, Pallas kernels: 14.2 us -> 13.6 us  [band(): pl.pallas_call(functools.partial(band_kernel, shifts, q_sizes, chained, s...]
  transfers between devices with their start and end apart: 14 -> 14, of which waited for: 5 -> 6; matrix products, arithmetic and copies ran while one was open for 1% -> 1% of each run, Pallas kernels for 35% -> 33%
where the time goes in v2:
time: 53.5 us; the launch traced here: 52.5 us
  starting transfers between devices  20.7 us (39%)
  Pallas kernels  20.1 us (38%)
  waiting for transfers between devices  9.47 us (18%)
  local copies, waits for them, and re-layouts  1.41 us (3%)
  between operations  0.78 us (1%)
    pallas_call x4, Pallas kernels, band(): pl.pallas_call(functools.partial(band_kernel, shifts, q_sizes, chained, s...  13.6 us
    ppermute x3, starting transfers between devices, down(): lax.ppermute(x, 'kcol', [(i + 2 * d, i) for i in range(col_count - 2 * d)])  7.67 us
    ppermute x6, starting transfers between devices, across(): lax.ppermute(x, 'qrow', [(i, i ^ j) for i in range(row_count)])  7.04 us
    ppermute x6, waiting for transfers between devices, across(): lax.ppermute(x, 'qrow', [(i, i ^ j) for i in range(row_count)])  4.59 us
    ppermute x3, waiting for transfers between devices, down(): lax.ppermute(x, 'kcol', [(i + 2 * d, i) for i in range(col_count - 2 * d)])  4.39 us
    ppermute x3, starting transfers between devices, up(): lax.ppermute(x, 'kcol', [(i, (i + 2 * d) % col_count) for i in range(col_...  4.05 us
    pallas_call x1, Pallas kernels, per_device(): pl.pallas_call(prep_kernel, in_specs=[VMEM_SPEC] * 4, out_specs=VMEM_SPEC...  2.31 us
    ppermute x2, starting transfers between devices, swap(): return lax.ppermute(x, 'kcol', [(i, i ^ 1) for i in range(col_count)])  1.92 us
  transfers between devices with their start and end apart: 14, of which 6 were waited for; matrix products, arithmetic and copies ran while one was open for 1% of the time, Pallas kernels for 33%

profile of v2, /device:TPU:16, one launch (start us, length us, event | category | flops | bytes accessed | tf_op | source)
XLA Modules:
  0.0 52.5 jit_solution(15724630467048993289)
XLA Ops:
  0.6 1.6 %pack.1 = (bf16[128,128]{1,0:T(8,128)(2,1)}, bf16[128,128]{1,0:T(8,128)(2,1)}, bf16[128,128]{1,0:T(8,128)(2,1)}, bf16[128,128]{1,0:T(8,128)(2,1)}) custom-call(s32[1]{0:T(128)} %bitcast.place, bf16[128,256]{1,0:T(8,128)(2,1)} %key.1, bf16[128,256]{1,0:T(8,128)(2,1)} %value.1), custom_call_target="tpu_custom_call" | custom-call | tf_op jit(solution)/shard_map/pack/pallas_call | solution.py:287
  2.3 1.5 %collective-permute-start = (bf16[128,128]{1,0:T(8,128)(2,1)}, bf16[128,128]{1,0:T(8,128)(2,1)S(1)}, u32[]{:S(2)}, u32[]{:S(2)}) collective-permute-start(bf16[128,128]{1,0:T(8,128)(2,1)} %get-tuple-element.41), channel_id=1, source_target_pairs={{0,8},{8,0},{16,24},{24,16},{1,9},{9,1},{17,25},{25,17},{2,10},{10... | collective-permute-start | bytes 98312 | tf_op jit(solution)/shard_map/ppermute | solution.py:284
  3.7 1.5 %collective-permute-start.1 = (bf16[128,128]{1,0:T(8,128)(2,1)}, bf16[128,128]{1,0:T(8,128)(2,1)S(1)}, u32[]{:S(2)}, u32[]{:S(2)}) collective-permute-start(bf16[128,128]{1,0:T(8,128)(2,1)} %get-tuple-element.42), channel_id=1, source_target_pairs={{0,16},{8,24},{16,0},{24,8},{1,17},{9,25},{17,1},{25,9},{2,18},{10... | collective-permute-start | bytes 98312 | tf_op jit(solution)/shard_map/ppermute | solution.py:284
  5.3 0.0 copy-start.1
  5.3 0.5 collective-permute-start.2
  5.7 2.3 %prep.1.refs_0_ = bf16[512,640]{1,0:T(8,128)(2,1)} custom-call(bf16[512,256]{1,0:T(8,128)(2,1)} %query.1, bf16[512,256]{1,0:T(8,128)(2,1)} %grad_out.1, bf16[512,256]{1,0:T(8,128)(2,1)} %output.1, f32[4,512]{1,0:T(4,128)} %lse.1), custom_call_target="tpu_custom_call" | custom-call | tf_op jit(solution)/shard_map/prep/pallas_call | solution.py:296
  8.1 0.0 collective-permute-done.refs_1_
  8.1 0.0 collective-permute-done.1.refs_2_
  8.1 2.2 %collective-permute-done.2.refs_3_ = bf16[128,128]{1,0:T(8,128)(2,1)S(1)} collective-permute-done((bf16[128,128]{1,0:T(8,128)(2,1)}, bf16[128,128]{1,0:T(8,128)(2,1)S(1)}, u32[]{:S(2)}, u32[]{:S(2)}) %collective-permute-start.2) | collective-permute-done | bytes 32800 | tf_op jit(solution)/shard_map/ppermute | solution.py:284
  10.3 0.0 collective-permute-start.3
  10.3 0.0 copy-done.1
  10.3 0.0 copy-start.2
  10.3 0.5 collective-permute-start.6
  10.8 3.5 %collective-permute-start.5 = (bf16[512,128]{1,0:T(8,128)(2,1)S(1)}, bf16[512,128]{1,0:T(8,128)(2,1)S(1)}, u32[]{:S(2)}, u32[]{:S(2)}) collective-permute-start(bf16[512,128]{1,0:T(8,128)(2,1)S(1)} %join.1.refs_8_), channel_id=1, source_target_pairs={{0,4},{1,5},{2,6},{3,7},{4,0},{5,1},{6,2},{7,3},{8,12},{9,13},{10,... | collective-permute-start | bytes 393224 | tf_op jit(solution)/shard_map/ppermute | solution.py:278
  14.3 0.1 pad_add_fusion.panel.refs_0_
  14.4 0.0 copy-done.2
  14.4 0.1 slice.7
  14.5 0.1 slice.6
  14.6 0.1 reshape.17.last.refs_2_
  14.6 0.1 reshape.16.first.refs_1_
  14.7 0.0 collective-permute-done.3.refs_1_
  14.7 0.0 copy-start
  14.7 1.1 %copy-done = bf16[512,640]{1,0:T(8,128)(2,1)S(1)} copy-done((bf16[512,640]{1,0:T(8,128)(2,1)S(1)}, bf16[512,640]{1,0:T(8,128)(2,1)}, u32[]{:S(2)}) %copy-start) | copy-done | bytes 655384
  15.8 1.4 %expand.1 = (bf16[4,1024,128]{2,1,0:T(8,128)(2,1)S(1)}, bf16[4,1024,128]{2,1,0:T(8,128)(2,1)S(1)}, bf16[256,1024]{1,0:T(8,128)(2,1)S(1)}, bf16[256,1024]{1,0:T(8,128)(2,1)S(1)}, s32[8,512]{1,0:T(8,128)S(1)}) custom-call(s32[2]{0:T(128)S(1)} %pad_add_fusion.panel.refs_0_, s32[16]{0:T(128)S(1)} %reshape.16.first.refs_1_, s32[16]{0:T(128)S(1)} %reshape.17.last.refs_2_, ...), custom_call_target="tpu_custom_call" | custom-call | tf_op jit(solution)/shard_map/expand/pallas_call | solution.py:312
  17.2 3.3 %own.1 = (f32[1024,256]{1,0:T(8,128)S(1)}, f32[128,512]{1,0:T(8,128)S(1)}) custom-call(s32[2]{0:T(128)S(1)} %pad_add_fusion.panel.refs_0_, s32[16]{0:T(128)S(1)} %reshape.16.first.refs_1_, s32[16]{0:T(128)S(1)} %reshape.17.last.refs_2_, bf16[4,1024,128]{2,1,0:T(8,128)(2,1)S(1)} %get-tuple-element.45.refs_3_, ...), custom_call_target="tpu_custom_call" | custom-call | flops 1342177280 | bytes 6291456 | tf_op jit(solution)/shard_map/own/pallas_call | solution.py:335
  20.5 0.1 collective-permute-start.4
  20.6 0.0 collective-permute-done.6.refs_9_
  20.6 0.5 collective-permute-done.5.refs_8_
  21.1 0.6 %far.1 = (f32[1024,256]{1,0:T(8,128)S(1)}, bf16[128,512]{1,0:T(8,128)(2,1)S(1)}, bf16[128,512]{1,0:T(8,128)(2,1)S(1)}) custom-call(s32[2]{0:T(128)S(1)} %pad_add_fusion.panel.refs_0_, s32[16]{0:T(128)S(1)} %reshape.16.first.refs_1_, s32[16]{0:T(128)S(1)} %reshape.17.last.refs_2_, ...), custom_call_target="tpu_custom_call", output_to_operand_aliasing={{0}: (10, {})} | custom-call | flops 2684354560 | bytes 6291456 | tf_op jit(solution)/shard_map/far/pallas_call | solution.py:335
  21.7 0.7 %collective-permute-start.7 = (bf16[128,512]{1,0:T(8,128)(2,1)S(1)}, bf16[128,512]{1,0:T(8,128)(2,1)S(1)}, u32[]{:S(2)}, u32[]{:S(2)}) collective-permute-start(bf16[128,512]{1,0:T(8,128)(2,1)S(1)} %get-tuple-element.59), channel_id=1, source_target_pairs={{6,0},{7,1},{14,8},{15,9},{22,16},{23,17},{30,24},{31,25}} | collective-permute-start | bytes 393224 | tf_op jit(solution)/shard_map/ppermute | solution.py:281
  22.4 5.1 %collective-permute-start.8 = (bf16[128,512]{1,0:T(8,128)(2,1)S(1)}, bf16[128,512]{1,0:T(8,128)(2,1)S(1)}, u32[]{:S(2)}, u32[]{:S(2)}) collective-permute-start(bf16[128,512]{1,0:T(8,128)(2,1)S(1)} %get-tuple-element.65), channel_id=1, source_target_pairs={{4,0},{5,1},{6,2},{7,3},{12,8},{13,9},{14,10},{15,11},{20,16},{21,... | collective-permute-start | bytes 393224 | tf_op jit(solution)/shard_map/ppermute | solution.py:281
  27.5 0.0 collective-permute-done.4.refs_8_
  27.5 6.1 %near.1 = (f32[1024,256]{1,0:T(8,128)S(1)}, bf16[128,512]{1,0:T(8,128)(2,1)S(1)}) custom-call(s32[2]{0:T(128)S(1)} %pad_add_fusion.panel.refs_0_, s32[16]{0:T(128)S(1)} %reshape.16.first.refs_1_, s32[16]{0:T(128)S(1)} %reshape.17.last.refs_2_, bf16[4,1024,128]{2,1,0:T(8,128)(2,1)S(1)} %get-tuple-element.45.refs_3_, ...), custom_call_target="tpu_custom_call", output_to_operand_aliasing={{0}: (9, {})} | custom-call | flops 1342177280 | bytes 6291456 | tf_op jit(solution)/shard_map/near/pallas_call | solution.py:335
  33.6 1.9 %collective-permute-start.9 = (bf16[128,512]{1,0:T(8,128)(2,1)S(1)}, bf16[128,512]{1,0:T(8,128)(2,1)S(1)}, u32[]{:S(2)}, u32[]{:S(2)}) collective-permute-start(bf16[128,512]{1,0:T(8,128)(2,1)S(1)} %get-tuple-element.67), channel_id=1, source_target_pairs={{2,0},{3,1},{4,2},{5,3},{6,4},{7,5},{10,8},{11,9},{12,10},{13,11},... | collective-permute-start | bytes 393224 | tf_op jit(solution)/shard_map/ppermute | solution.py:281
  35.5 0.0 collective-permute-done.7.refs_3_
  35.5 3.6 %rest.1 = (f32[1024,256]{1,0:T(8,128)S(1)}, f32[128,512]{1,0:T(8,128)S(1)}, bf16[512,256]{1,0:T(8,128)(2,1)S(1)}) custom-call(s32[2]{0:T(128)S(1)} %pad_add_fusion.panel.refs_0_, s32[16]{0:T(128)S(1)} %reshape.16.first.refs_1_, s32[16]{0:T(128)S(1)} %reshape.17.last.refs_2_, ...), custom_call_target="tpu_custom_call", output_to_operand_aliasing={{0}: (9, {})} | custom-call | flops 1342177280 | bytes 6291456 | tf_op jit(solution)/shard_map/rest/pallas_call | solution.py:335
  39.1 0.0 collective-permute-done.8.refs_2_
  39.1 4.4 %collective-permute-done.9.refs_4_ = bf16[128,512]{1,0:T(8,128)(2,1)S(1)} collective-permute-done((bf16[128,512]{1,0:T(8,128)(2,1)S(1)}, bf16[128,512]{1,0:T(8,128)(2,1)S(1)}, u32[]{:S(2)}, u32[]{:S(2)}) %collective-permute-start.9) | collective-permute-done | bytes 131104 | tf_op jit(solution)/shard_map/ppermute | solution.py:281
  43.5 1.9 %collective-permute-start.13 = (bf16[512,256]{1,0:T(8,128)(2,1)S(1)}, bf16[512,256]{1,0:T(8,128)(2,1)S(1)}, u32[]{:S(2)}, u32[]{:S(2)}) collective-permute-start(bf16[512,256]{1,0:T(8,128)(2,1)S(1)} %get-tuple-element.76), channel_id=1, source_target_pairs={{0,1},{1,0},{2,3},{3,2},{4,5},{5,4},{6,7},{7,6},{8,9},{9,8},{10,11... | collective-permute-start | bytes 786440 | tf_op jit(solution)/shard_map/ppermute | solution.py:275
  45.4 0.1 collect.1
  45.6 0.6 %collective-permute-start.10 = (bf16[128,128]{1,0:T(8,128)(2,1)S(1)}, bf16[128,128]{1,0:T(8,128)(2,1)S(1)}, u32[]{:S(2)}, u32[]{:S(2)}) collective-permute-start(bf16[128,128]{1,0:T(8,128)(2,1)S(1)} %get-tuple-element.73), channel_id=1, source_target_pairs={{0,8},{8,0},{16,24},{24,16},{1,9},{9,1},{17,25},{25,17},{2,10},{10... | collective-permute-start | bytes 98312 | tf_op jit(solution)/shard_map/ppermute | solution.py:284
  46.2 0.5 collective-permute-start.11
  46.7 2.5 %collective-permute-start.12 = (bf16[128,128]{1,0:T(8,128)(2,1)S(1)}, bf16[128,128]{1,0:T(8,128)(2,1)S(1)}, u32[]{:S(2)}, u32[]{:S(2)}) collective-permute-start(bf16[128,128]{1,0:T(8,128)(2,1)S(1)} %get-tuple-element.75), channel_id=1, source_target_pairs={{0,24},{8,16},{16,8},{24,0},{1,25},{9,17},{17,9},{25,1},{2,26},{10... | collective-permute-start | bytes 98312 | tf_op jit(solution)/shard_map/ppermute | solution.py:284
  49.1 0.4 collective-permute-done.10.refs_1_
  49.5 0.8 %collective-permute-done.11.refs_2_ = bf16[128,128]{1,0:T(8,128)(2,1)S(1)} collective-permute-done((bf16[128,128]{1,0:T(8,128)(2,1)S(1)}, bf16[128,128]{1,0:T(8,128)(2,1)S(1)}, u32[]{:S(2)}, u32[]{:S(2)}) %collective-permute-start.11) | collective-permute-done | bytes 32800 | tf_op jit(solution)/shard_map/ppermute | solution.py:284
  50.3 1.2 %collective-permute-done.12.refs_3_ = bf16[128,128]{1,0:T(8,128)(2,1)S(1)} collective-permute-done((bf16[128,128]{1,0:T(8,128)(2,1)S(1)}, bf16[128,128]{1,0:T(8,128)(2,1)S(1)}, u32[]{:S(2)}, u32[]{:S(2)}) %collective-permute-start.12) | collective-permute-done | bytes 32800 | tf_op jit(solution)/shard_map/ppermute | solution.py:284
  51.5 0.0 collective-permute-done.13.refs_4_
  51.5 1.0 %finish.1 = (f32[512,256]{1,0:T(8,128)}, f32[128,256]{1,0:T(8,128)}, f32[128,256]{1,0:T(8,128)}) custom-call(s32[1]{0:T(128)} %bitcast.place, f32[1024,256]{1,0:T(8,128)S(1)} %get-tuple-element.61.dq, bf16[128,128]{1,0:T(8,128)(2,1)S(1)} %get-tuple-element.72.refs_0_, bf16[128,128]{1,0:T(8,128)(2,1)S(1)} %collective-permute-done.10.refs_1_, ...), custom_call_target="tpu_custom_call" | custom-call | tf_op jit(solution)/shard_map/finish/pallas_call | solution.py:384
  (2 shorter events, 0.0 us)
Async XLA Ops:
  2.3 5.8 %collective-permute-start = (bf16[128,128]{1,0:T(8,128)(2,1)}, bf16[128,128]{1,0:T(8,128)(2,1)S(1)}, u32[]{:S(2)}, u32[]{:S(2)}) collective-permute-start(bf16[128,128]{1,0:T(8,128)(2,1)} %get-tuple-element.41), channel_id=1, source_target_pairs={{0,8},{8,0},{16,24},{24,16},{1,9},{9,1},{17,25},{25,17},{2,10},{10... | collective-permute-start | bytes 98312 | tf_op jit(solution)/shard_map/ppermute | solution.py:284
  3.7 4.3 %collective-permute-start.1 = (bf16[128,128]{1,0:T(8,128)(2,1)}, bf16[128,128]{1,0:T(8,128)(2,1)S(1)}, u32[]{:S(2)}, u32[]{:S(2)}) collective-permute-start(bf16[128,128]{1,0:T(8,128)(2,1)} %get-tuple-element.42), channel_id=1, source_target_pairs={{0,16},{8,24},{16,0},{24,8},{1,17},{9,25},{17,1},{25,9},{2,18},{10... | collective-permute-start | bytes 98312 | tf_op jit(solution)/shard_map/ppermute | solution.py:284
  5.3 5.0 %copy-start.1 = (bf16[128,128]{1,0:T(8,128)(2,1)S(1)}, bf16[128,128]{1,0:T(8,128)(2,1)}, u32[]{:S(2)}) copy-start(bf16[128,128]{1,0:T(8,128)(2,1)} %get-tuple-element.50.refs_0_) | copy-start | bytes 98308
  5.3 5.0 %collective-permute-start.2 = (bf16[128,128]{1,0:T(8,128)(2,1)}, bf16[128,128]{1,0:T(8,128)(2,1)S(1)}, u32[]{:S(2)}, u32[]{:S(2)}) collective-permute-start(bf16[128,128]{1,0:T(8,128)(2,1)} %get-tuple-element.43), channel_id=1, source_target_pairs={{0,24},{8,16},{16,8},{24,0},{1,25},{9,17},{17,9},{25,1},{2,26},{10... | collective-permute-start | bytes 98312 | tf_op jit(solution)/shard_map/ppermute | solution.py:284
  10.3 4.4 %collective-permute-start.3 = (bf16[512,640]{1,0:T(8,128)(2,1)}, bf16[512,640]{1,0:T(8,128)(2,1)S(1)}, u32[]{:S(2)}, u32[]{:S(2)}) collective-permute-start(bf16[512,640]{1,0:T(8,128)(2,1)} %prep.1.refs_0_), channel_id=1, source_target_pairs={{0,1},{1,0},{2,3},{3,2},{4,5},{5,4},{6,7},{7,6},{8,9},{9,8},{10,11... | collective-permute-start | bytes 1966088 | tf_op jit(solution)/shard_map/ppermute | solution.py:275
  10.3 4.1 %copy-start.2 = (s32[4096]{0:T(1024)S(1)}, s32[4096]{0:T(1024)}, u32[]{:S(2)}) copy-start(s32[4096]{0:T(1024)} %param.13) | copy-start | bytes 49156
  10.3 10.3 %collective-permute-start.6 = (bf16[512,128]{1,0:T(8,128)(2,1)S(1)}, bf16[512,128]{1,0:T(8,128)(2,1)S(1)}, u32[]{:S(2)}, u32[]{:S(2)}) collective-permute-start(bf16[512,128]{1,0:T(8,128)(2,1)S(1)} %join.1.refs_8_), channel_id=1, source_target_pairs={{0,6},{1,7},{2,0},{3,1},{4,2},{5,3},{6,4},{7,5},{8,14},{9,15},{10,... | collective-permute-start | bytes 393224 | tf_op jit(solution)/shard_map/ppermute | solution.py:278
  10.8 10.3 %collective-permute-start.5 = (bf16[512,128]{1,0:T(8,128)(2,1)S(1)}, bf16[512,128]{1,0:T(8,128)(2,1)S(1)}, u32[]{:S(2)}, u32[]{:S(2)}) collective-permute-start(bf16[512,128]{1,0:T(8,128)(2,1)S(1)} %join.1.refs_8_), channel_id=1, source_target_pairs={{0,4},{1,5},{2,6},{3,7},{4,0},{5,1},{6,2},{7,3},{8,12},{9,13},{10,... | collective-permute-start | bytes 393224 | tf_op jit(solution)/shard_map/ppermute | solution.py:278
  14.7 1.1 %copy-start = (bf16[512,640]{1,0:T(8,128)(2,1)S(1)}, bf16[512,640]{1,0:T(8,128)(2,1)}, u32[]{:S(2)}) copy-start(bf16[512,640]{1,0:T(8,128)(2,1)} %prep.1.refs_0_) | copy-start | bytes 1966084
  20.5 6.9 %collective-permute-start.4 = (bf16[512,128]{1,0:T(8,128)(2,1)S(1)}, bf16[512,128]{1,0:T(8,128)(2,1)S(1)}, u32[]{:S(2)}, u32[]{:S(2)}) collective-permute-start(bf16[512,128]{1,0:T(8,128)(2,1)S(1)} %join.1.refs_8_), channel_id=1, source_target_pairs={{0,2},{1,3},{2,4},{3,5},{4,6},{5,7},{6,0},{7,1},{8,10},{9,11},{10,... | collective-permute-start | bytes 393224 | tf_op jit(solution)/shard_map/ppermute | solution.py:278
  21.7 13.8 %collective-permute-start.7 = (bf16[128,512]{1,0:T(8,128)(2,1)S(1)}, bf16[128,512]{1,0:T(8,128)(2,1)S(1)}, u32[]{:S(2)}, u32[]{:S(2)}) collective-permute-start(bf16[128,512]{1,0:T(8,128)(2,1)S(1)} %get-tuple-element.59), channel_id=1, source_target_pairs={{6,0},{7,1},{14,8},{15,9},{22,16},{23,17},{30,24},{31,25}} | collective-permute-start | bytes 393224 | tf_op jit(solution)/shard_map/ppermute | solution.py:281
  22.4 16.7 %collective-permute-start.8 = (bf16[128,512]{1,0:T(8,128)(2,1)S(1)}, bf16[128,512]{1,0:T(8,128)(2,1)S(1)}, u32[]{:S(2)}, u32[]{:S(2)}) collective-permute-start(bf16[128,512]{1,0:T(8,128)(2,1)S(1)} %get-tuple-element.65), channel_id=1, source_target_pairs={{4,0},{5,1},{6,2},{7,3},{12,8},{13,9},{14,10},{15,11},{20,16},{21,... | collective-permute-start | bytes 393224 | tf_op jit(solution)/shard_map/ppermute | solution.py:281
  33.6 9.9 %collective-permute-start.9 = (bf16[128,512]{1,0:T(8,128)(2,1)S(1)}, bf16[128,512]{1,0:T(8,128)(2,1)S(1)}, u32[]{:S(2)}, u32[]{:S(2)}) collective-permute-start(bf16[128,512]{1,0:T(8,128)(2,1)S(1)} %get-tuple-element.67), channel_id=1, source_target_pairs={{2,0},{3,1},{4,2},{5,3},{6,4},{7,5},{10,8},{11,9},{12,10},{13,11},... | collective-permute-start | bytes 393224 | tf_op jit(solution)/shard_map/ppermute | solution.py:281
  43.5 8.0 %collective-permute-start.13 = (bf16[512,256]{1,0:T(8,128)(2,1)S(1)}, bf16[512,256]{1,0:T(8,128)(2,1)S(1)}, u32[]{:S(2)}, u32[]{:S(2)}) collective-permute-start(bf16[512,256]{1,0:T(8,128)(2,1)S(1)} %get-tuple-element.76), channel_id=1, source_target_pairs={{0,1},{1,0},{2,3},{3,2},{4,5},{5,4},{6,7},{7,6},{8,9},{9,8},{10,11... | collective-permute-start | bytes 786440 | tf_op jit(solution)/shard_map/ppermute | solution.py:275
  45.6 4.0 %collective-permute-start.10 = (bf16[128,128]{1,0:T(8,128)(2,1)S(1)}, bf16[128,128]{1,0:T(8,128)(2,1)S(1)}, u32[]{:S(2)}, u32[]{:S(2)}) collective-permute-start(bf16[128,128]{1,0:T(8,128)(2,1)S(1)} %get-tuple-element.73), channel_id=1, source_target_pairs={{0,8},{8,0},{16,24},{24,16},{1,9},{9,1},{17,25},{25,17},{2,10},{10... | collective-permute-start | bytes 98312 | tf_op jit(solution)/shard_map/ppermute | solution.py:284
  46.2 4.1 %collective-permute-start.11 = (bf16[128,128]{1,0:T(8,128)(2,1)S(1)}, bf16[128,128]{1,0:T(8,128)(2,1)S(1)}, u32[]{:S(2)}, u32[]{:S(2)}) collective-permute-start(bf16[128,128]{1,0:T(8,128)(2,1)S(1)} %get-tuple-element.74), channel_id=1, source_target_pairs={{0,16},{8,24},{16,0},{24,8},{1,17},{9,25},{17,1},{25,9},{2,18},{10... | collective-permute-start | bytes 98312 | tf_op jit(solution)/shard_map/ppermute | solution.py:284
  46.7 4.8 %collective-permute-start.12 = (bf16[128,128]{1,0:T(8,128)(2,1)S(1)}, bf16[128,128]{1,0:T(8,128)(2,1)S(1)}, u32[]{:S(2)}, u32[]{:S(2)}) collective-permute-start(bf16[128,128]{1,0:T(8,128)(2,1)S(1)} %get-tuple-element.75), channel_id=1, source_target_pairs={{0,24},{8,16},{16,8},{24,0},{1,25},{9,17},{17,9},{25,1},{2,26},{10... | collective-permute-start | bytes 98312 | tf_op jit(solution)/shard_map/ppermute | solution.py:284
